TPU v7x, 32 devices: a whole 2x2x4 slice. The times are simulated.
32 devices in a mesh: groups: 2 (over x), slab: 4 (over y, core), view: 4 (over z).
Axes of the slice: x: 2, y: 2, z: 4, core: 2. Of those that a mesh axis runs over, the one named last changes fastest.
Arguments:
- estimate: float32 [128, 64, 256], P(('groups', 'slab')), parts along dimension 0, may hold values from 0.3 to 3
- measured: float32 [8, 128, 64, 256], P('view', ('groups', 'slab')), parts along dimension 1, may hold values from 0.2 to 5
- psf_z: float32 [8, 4, 15], P('view'), may hold values from 0.01 to 1
- psf_y: float32 [8, 4, 15], P('view'), may hold values from 0.01 to 1
- psf_x: float32 [8, 4, 15], P('view'), may hold values from 0.01 to 1
- weight_table: float32 [4], replicated, may hold values from 0.1 to 1
- weight_index: int32 [8], replicated, may hold values from 0 to 3
Outputs:
- new_estimate: float32 [128, 64, 256], P(('groups', 'slab')), parts along dimension 0
There are 2 independent parts, one for each index of `groups`. A program takes and returns all parts, laid end to end along the dimension named above; an argument that names none is the same for every part. Nothing has to cross between parts.
All inputs are finite; a program needn't handle non-finite values.
Results may differ from a plain program's by a relative error of at most 0.000068.
Values sent between devices are 32-bit elements; how exact they have to be, the bound alone decides.
No kernel may reach another device: no remote copies, remote signals or barrier semaphores. Data moves between devices by JAX's collectives and lax.ppermute only.
A program may use at most 64 MiB of HBM per device.

v0:
```python
import functools

import jax
import jax.numpy as jnp
from jax import lax
from jax.experimental import pallas as pl
from jax.experimental.pallas import tpu as pltpu
from jax.sharding import PartitionSpec as P

f32 = jnp.float32
bf16 = jnp.bfloat16
SUB = 8
VMEM_LIMIT = 24 * 2**20


def split(values):
    high = values.astype(bf16)
    return high, (values - high.astype(f32)).astype(bf16)


def dot(a, b):
    return jnp.dot(a, b, preferred_element_type=f32)


def skew(row, rows, shift):
    width = row.shape[1]
    full = jnp.broadcast_to(row, (rows, width))
    return pltpu.roll(full, shift % width, 1, stride=1, stride_axis=0)


def tap_row(ref, place, width, start, step, flip):
    taps = ref.shape[-1]
    lane = lax.broadcasted_iota(jnp.int32, (1, width), 1)
    row = jnp.zeros((1, width), f32)
    for k in range(taps):
        value = ref[place + (taps - 1 - k if flip else k,)]
        row = jnp.where(lane == start + k * step, value, row)
    return row


def prep_kernel(chunk, psf_z, psf_y, psf_x, table, index, est, xh, xl, ym, zm, scale):
    members, rank, taps = psf_x.shape
    planes, height, width = est.shape
    radius = (taps - 1) // 2
    packed = rank * height
    first = lax.axis_index("slab") * planes
    total = lax.axis_size("slab") * planes
    view = lax.axis_index("view")

    def weight_of(v):
        code = index[v]
        weight = jnp.float32(0)
        for level in range(table.shape[0]):
            weight = weight + jnp.where(code == level, table[level], jnp.float32(0))
        return weight

    grand = jnp.float32(0)
    for v in range(index.shape[0]):
        grand = grand + weight_of(v)
    q = lax.broadcasted_iota(jnp.int32, (width, width), 0)
    p = lax.broadcasted_iota(jnp.int32, (width, width), 1)
    band = jnp.abs(p - q) <= radius
    yp = lax.broadcasted_iota(jnp.int32, (height, packed), 0)
    lane = lax.broadcasted_iota(jnp.int32, (height, packed), 1)
    yband = jnp.abs(lax.rem(lane, height) - yp) <= radius
    depth = first + lax.broadcasted_iota(jnp.int32, (planes, width), 0)
    for m in range(members):
        for way in range(2):
            slot = 2 * m + way
            flip = way == 0
            col_x = []
            for r in range(rank):
                mat = jnp.where(band, skew(tap_row(psf_x, (m, r), width, 0, 1, flip), width, -radius), 0.0)
                high, low = split(mat)
                xh[slot, r] = high
                xl[slot, r] = low
                if way:
                    col_x.append(jnp.sum(mat, axis=0, keepdims=True))
            row = jnp.zeros((1, packed), f32)
            for r in range(rank):
                row = row + tap_row(psf_y, (m, r), packed, r * height, 1, not flip)
            ymat = jnp.where(yband, skew(row, height, -radius), 0.0)
            high, low = split(ymat)
            ym[slot] = jnp.concatenate([high, low], axis=0)
            zmat = jnp.concatenate(
                [skew(tap_row(psf_z, (m, r), zm.shape[2], 0, SUB, not flip), chunk * SUB, 0) for r in range(rank)],
                axis=0,
            )
            high, low = split(zmat)
            zm[slot] = jnp.concatenate([high, low], axis=0)
        shares = []
        for r in range(rank):
            own = (lane >= r * height) & (lane < (r + 1) * height)
            col_y = jnp.sum(jnp.where(own, ymat, 0.0), axis=1, keepdims=True)
            col_z = jnp.zeros((planes, width), f32)
            for k in range(taps):
                source = depth + (radius - k)
                inside = (source >= 0) & (source < total)
                col_z = col_z + jnp.where(inside, psf_z[m, r, k], 0.0)
            shares.append((col_z, col_y * col_x[r]))
        weight = weight_of(view * members + m)
        for z in range(planes):
            normal = jnp.zeros((height, width), f32)
            for col_z, outer in shares:
                normal = normal + col_z[z : z + 1] * outer
            scale[m, z] = est[z] * (weight / (grand * normal))


def load_split(pieces, first, last, high, low):
    starts = [0]
    for piece in pieces:
        starts.append(starts[-1] + piece.shape[0])
    for block in range(high.shape[0]):
        parts = []
        for piece, start in zip(pieces, starts):
            a, b = max(first - start, 0), min(last - start, piece.shape[0])
            if a < b:
                parts.append(piece[a:b, block * SUB : (block + 1) * SUB, :])
        rows = jnp.concatenate(parts, axis=0)
        rows = rows.reshape((last - first) * SUB, rows.shape[2])
        h, l = split(rows)
        high[block, 0 : rows.shape[0]] = h
        low[block, 0 : rows.shape[0]] = l


def apply_chunk(c, chunk, reach, high, low, mats, scratch):
    xh, xl, ym, zm = mats
    dh, dl, f = scratch
    rank, width = xh.shape[0], xh.shape[1]
    blocks = high.shape[0]
    height = blocks * SUB
    depth = (chunk + reach) * SUB
    rows = chunk * SUB
    stacked = rank * rows
    zmat = zm[:, 0:depth]
    window = pl.ds(c * rows if isinstance(c, int) else pl.multiple_of(c * rows, rows), depth)
    for block in range(blocks):
        hw = high[block, window, :]
        lw = low[block, window, :]
        both = dot(zmat, hw)
        d = both[:stacked] + both[stacked:] + dot(zmat[:stacked], lw)
        for r in range(rank):
            h, l = split(d[r * rows : (r + 1) * rows])
            dh[r, block * rows : (block + 1) * rows] = h
            dl[r, block * rows : (block + 1) * rows] = l
    for r in range(rank):
        f[r] = dot(dh[r], xh[r]) + dot(dl[r], xh[r]) + dot(dh[r], xl[r])
    results = []
    for z in range(chunk):
        plane = [f[r].reshape(blocks, chunk, SUB, width)[:, z].reshape(height, width) for r in range(rank)]
        h, l = split(jnp.concatenate(plane, axis=0))
        both = dot(ym[...], h)
        results.append(both[:height] + both[height:] + dot(ym[0:height], l))
    return results


def forward_kernel(chunk, reach, before, est, after, measured, *rest):
    mats, (ratio, head, tail, high, low, *scratch) = rest[:4], rest[4:]
    c = pl.program_id(0)
    planes = ratio.shape[0]

    @pl.when(c == 0)
    def _():
        load_split((before, est, after), 0, planes + reach, high, low)

    blurred = apply_chunk(c, chunk, reach, high, low, mats, scratch)
    for z in range(chunk):
        ratio[c * chunk + z] = measured[z] / blurred[z]

    @pl.when(c == pl.num_programs(0) - 1)
    def _():
        head[...] = ratio[0 : head.shape[0]]
        tail[...] = ratio[planes - tail.shape[0] : planes]


def backward_kernel(chunk, reach, first, count, views, has_sum, has_after, *refs):
    refs = list(refs)
    take = lambda n: [refs.pop(0) for _ in range(n)]
    per_view = [(take(3), take(1)[0], take(4)) for _ in range(views)]
    running = take(1)[0] if has_sum else None
    if has_after:
        take(1)
    (out,) = take(1)
    high, low, *scratch = refs
    for i, (pieces, scale, mats) in enumerate(per_view):
        load_split(pieces, first * chunk, (first + count) * chunk + reach, high, low)
        for c in range(count):
            back = apply_chunk(c, chunk, reach, high, low, mats, scratch)
            for z in range(chunk):
                term = back[z] * scale[c * chunk + z]
                if i:
                    term = term + out[c * chunk + z]
                elif has_sum:
                    term = term + running[z]
                out[c * chunk + z] = term


def whole(shape):
    return pl.BlockSpec(shape, lambda *_: (0,) * len(shape))


def slot_of(array, slot):
    return pl.BlockSpec((None,) + array.shape[1:], lambda *_: (slot,) + (0,) * (array.ndim - 1))


def per_device(estimate, measured, psf_z, psf_y, psf_x, weight_table, weight_index):
    members, planes, height, width = measured.shape
    rank, taps = psf_x.shape[1:]
    reach = taps - 1
    radius = reach // 2
    chunk = next(c for c in (4, 2, 1) if planes % c == 0)
    chunks = planes // chunk
    struct = jax.ShapeDtypeStruct
    plane = (height, width)
    params = pltpu.CompilerParams(vmem_limit_bytes=VMEM_LIMIT)
    smem = pl.BlockSpec(memory_space=pltpu.SMEM)

    slabs = lax.axis_size("slab")
    up = [(i, i + 1) for i in range(slabs - 1)]
    down = [(i + 1, i) for i in range(slabs - 1)]

    def cost(fraction):
        flops = 2 * 6912 * 65536 * chunks * fraction
        return pl.CostEstimate(flops=int(flops), bytes_accessed=int(4e6), transcendentals=0)

    before = lax.ppermute(estimate[planes - radius :], "slab", up)
    after = lax.ppermute(estimate[:radius], "slab", down)
    depth_lanes = -(-(chunk + reach) * SUB // 128) * 128
    slots = 2 * members
    mats_and_scale = pl.pallas_call(
        functools.partial(prep_kernel, chunk),
        out_shape=[
            struct((slots, rank, width, width), bf16),
            struct((slots, rank, width, width), bf16),
            struct((slots, 2 * height, rank * height), bf16),
            struct((slots, 2 * rank * chunk * SUB, depth_lanes), bf16),
            struct((members, planes) + plane, f32),
        ],
        in_specs=[smem] * 5 + [pl.BlockSpec(memory_space=pltpu.VMEM)],
        compiler_params=params,
        cost_estimate=cost(0.7),
        name="prep",
    )(psf_z, psf_y, psf_x, weight_table, weight_index, estimate)
    mats, scale = mats_and_scale[:4], mats_and_scale[4]

    def work(window):
        return [
            pltpu.VMEM((height // SUB, window * SUB, width), bf16),
            pltpu.VMEM((height // SUB, window * SUB, width), bf16),
            pltpu.VMEM((rank, height * chunk, width), bf16),
            pltpu.VMEM((rank, height * chunk, width), bf16),
            pltpu.VMEM((rank, height * chunk, width), f32),
        ]

    extended = []
    for m in range(members):
        ratio, head, tail = pl.pallas_call(
            functools.partial(forward_kernel, chunk, reach),
            grid=(chunks,),
            out_shape=[struct((planes,) + plane, f32), struct((radius,) + plane, f32), struct((radius,) + plane, f32)],
            in_specs=[
                whole(before.shape),
                whole(estimate.shape),
                whole(after.shape),
                pl.BlockSpec((None, chunk) + plane, lambda c, m=m: (m, c, 0, 0)),
            ]
            + [slot_of(a, 2 * m) for a in mats],
            out_specs=[whole((planes,) + plane), whole((radius,) + plane), whole((radius,) + plane)],
            scratch_shapes=work(planes + reach),
            compiler_params=params,
            cost_estimate=cost(1),
            name=f"forward{m}",
        )(before, estimate, after, measured, *mats)
        extended.append((lax.ppermute(tail, "slab", up), ratio, lax.ppermute(head, "slab", down)))

    def backward(views, first, count, running, after, name):
        operands, specs = [], []
        for m in views:
            operands += list(extended[m]) + [scale] + list(mats)
            specs += [whole(a.shape) for a in extended[m]]
            if first % count:
                raise ValueError("chunk start")
            specs.append(pl.BlockSpec((None, count * chunk) + plane, lambda *_, m=m: (m, first // count, 0, 0)))
            specs += [slot_of(a, 2 * m + 1) for a in mats]
        if running is not None:
            source, place = running
            operands.append(source)
            specs.append(pl.BlockSpec((chunk,) + plane, lambda *_: (place, 0, 0)))
        if after is not None:
            operands.append(after)
            specs.append(pl.BlockSpec(memory_space=pl.ANY))
        return pl.pallas_call(
            functools.partial(backward_kernel, chunk, reach, first, count, len(views), running is not None, after is not None),
            grid=(1,),
            out_shape=struct((count * chunk,) + plane, f32),
            in_specs=specs,
            out_specs=whole((count * chunk,) + plane),
            scratch_shapes=work(count * chunk + reach),
            compiler_params=params,
            cost_estimate=cost(len(views) * count / chunks),
            name=name,
        )(*operands)

    early = min(2, chunks) if members > 1 else 0
    every = list(range(members))
    previous = None
    if early:
        previous = partial = backward(every[:-1], 0, early, None, None, "back_early")
    pieces = []
    for c in range(chunks):
        if c < early:
            previous = backward(every[-1:], c, 1, (partial, c), previous if c else None, f"back{c}")
        else:
            previous = backward(every, c, 1, None, previous, f"back{c}")
        pieces.append(previous)

    return jnp.concatenate([summed_over(piece, "view") for piece in pieces], axis=0)


def summed_over(piece, axis):
    count = lax.axis_size(axis)
    if count == 1:
        return piece
    if count % 2:
        return lax.psum(piece, axis)
    half = count // 2
    place = lax.axis_index(axis)
    for s in range(half - 1):
        piece = piece + lax.ppermute(piece, axis, [(s, s + 1), (count - 1 - s, count - 2 - s)])
    piece = piece + lax.ppermute(piece, axis, [(half - 1, half), (half, half - 1)])
    for s in range(half - 1):
        low, high = half - 2 - s, half + 1 + s
        moved = lax.ppermute(piece, axis, [(low + 1, low), (high - 1, high)])
        piece = jnp.where((place == low) | (place == high), moved, piece)
    return piece


def solution(mesh):
    placed = (
        P(("groups", "slab"), None, None),
        P("view", ("groups", "slab"), None, None),
        P("view", None, None),
        P("view", None, None),
        P("view", None, None),
        P(),
        P(),
    )
    return jax.shard_map(
        per_device,
        mesh=mesh,
        in_specs=placed,
        out_specs=P(("groups", "slab"), None, None),
        check_vma=False,
    )
```

profile of v0, /device:TPU:1, one launch (start us, length us, event | category | flops | bytes accessed | tf_op | source)
XLA Modules:
  0.0 100.4 jit_solution(7137119333420003013)
XLA Ops:
  0.0 1.2 %fusion = (f32[7,64,256]{2,1,0:T(8,128)S(1)}, f32[7,64,256]{2,1,0:T(8,128)S(1)}) fusion(f32[16,64,256]{2,1,0:T(8,128)} %est.5), kind=kLoop, calls=%fused_computation.5 | loop fusion | bytes 1835008 | tf_op jit(solution)/shard_map/slice | solution.py:227
  1.2 4.5 %collective-permute-start = (f32[7,64,256]{2,1,0:T(8,128)S(1)}, f32[7,64,256]{2,1,0:T(8,128)S(1)}, u32[]{:S(2)}, u32[]{:S(2)}) collective-permute-start(f32[7,64,256]{2,1,0:T(8,128)S(1)} %get-tuple-element.28), channel_id=1, source_target_pairs={{0,4},{4,8},{8,12},{1,5},{5,9},{9,13},{2,6},{6,10},{10,14},{3,7},{... | collective-permute-start | bytes 1376264 | tf_op jit(solution)/shard_map/ppermute | solution.py:226
  5.8 1.9 %collective-permute-start.1 = (f32[7,64,256]{2,1,0:T(8,128)S(1)}, f32[7,64,256]{2,1,0:T(8,128)S(1)}, u32[]{:S(2)}, u32[]{:S(2)}) collective-permute-start(f32[7,64,256]{2,1,0:T(8,128)S(1)} %get-tuple-element.27), channel_id=1, source_target_pairs={{4,0},{8,4},{12,8},{5,1},{9,5},{13,9},{6,2},{10,6},{14,10},{7,3},{... | collective-permute-start | bytes 1376264 | tf_op jit(solution)/shard_map/ppermute | solution.py:227
  7.7 0.0 copy-start
  7.7 1.2 %copy-done = f32[16,64,256]{2,1,0:T(8,128)S(1)} copy-done((f32[16,64,256]{2,1,0:T(8,128)S(1)}, f32[16,64,256]{2,1,0:T(8,128)}, u32[]{:S(2)}) %copy-start) | copy-done | bytes 1048600
  8.9 0.0 copy-start.2
  8.9 0.7 copy-done.2
  9.6 0.0 copy-start.3
  9.6 0.7 copy-done.3
  10.3 0.0 copy-start.4
  10.3 0.7 copy-done.4
  11.0 0.0 copy-start.5
  11.0 0.7 copy-done.5
  11.6 0.0 copy-start.6
  11.6 0.7 copy-done.6
  12.3 0.0 copy-start.1
  12.3 2.9 %prep.1 = (bf16[4,4,256,256]{3,2,1,0:T(8,128)(2,1)S(1)}, bf16[4,4,256,256]{3,2,1,0:T(8,128)(2,1)S(1)}, bf16[4,128,256]{2,1,0:T(8,128)(2,1)S(1)}, bf16[4,256,256]{2,1,0:T(8,128)(2,1)S(1)}, f32[2,16,64,256]{3,2,1,0:T(8,128)S(1)}) custom-call(f32[2,4,15]{2,1,0:T(4,128)S(1)} %copy-done.2, f32[2,4,15]{2,1,0:T(4,128)S(1)} %copy-done.3, f32[2,4,15]{2,1,0:T(4,128)S(1)} %copy-done.4, ...), custom_call_target="tpu_custom_call" | custom-call | flops 2536715008 | bytes 4000000 | tf_op jit(solution)/shard_map/prep/pallas_call | solution.py:230
  15.2 0.0 collective-permute-done.before
  15.2 0.4 collective-permute-done.1.after
  15.6 0.0 copy-done.1
  15.6 5.7 %forward0.1 = (f32[16,64,256]{2,1,0:T(8,128)S(1)}, f32[7,64,256]{2,1,0:T(8,128)S(1)}, f32[7,64,256]{2,1,0:T(8,128)S(1)}) custom-call(f32[7,64,256]{2,1,0:T(8,128)S(1)} %collective-permute-done.before, f32[16,64,256]{2,1,0:T(8,128)S(1)} %copy-done, f32[7,64,256]{2,1,0:T(8,128)S(1)} %collective-permute-done.1.after, f32[2,16,64,256]{3,2,1,0:T(8,128)S(1)} %copy-done.1, ...), custom_call_target="tpu_custom_call" | custom-call | flops 3623878656 | bytes 4000000 | tf_op jit(solution)/shard_map/forward0/pallas_call | solution.py:257
  21.2 3.3 %collective-permute-start.4 = (f32[7,64,256]{2,1,0:T(8,128)S(1)}, f32[7,64,256]{2,1,0:T(8,128)S(1)}, u32[]{:S(2)}, u32[]{:S(2)}) collective-permute-start(f32[7,64,256]{2,1,0:T(8,128)S(1)} %get-tuple-element.24), channel_id=1, source_target_pairs={{0,4},{4,8},{8,12},{1,5},{5,9},{9,13},{2,6},{6,10},{10,14},{3,7},{... | collective-permute-start | bytes 1376264 | tf_op jit(solution)/shard_map/ppermute | solution.py:274
  24.5 1.9 %collective-permute-start.5 = (f32[7,64,256]{2,1,0:T(8,128)S(1)}, f32[7,64,256]{2,1,0:T(8,128)S(1)}, u32[]{:S(2)}, u32[]{:S(2)}) collective-permute-start(f32[7,64,256]{2,1,0:T(8,128)S(1)} %get-tuple-element.26), channel_id=1, source_target_pairs={{4,0},{8,4},{12,8},{5,1},{9,5},{13,9},{6,2},{10,6},{14,10},{7,3},{... | collective-permute-start | bytes 1376264 | tf_op jit(solution)/shard_map/ppermute | solution.py:274
  26.5 5.7 %forward1.1 = (f32[16,64,256]{2,1,0:T(8,128)S(1)}, f32[7,64,256]{2,1,0:T(8,128)S(1)}, f32[7,64,256]{2,1,0:T(8,128)S(1)}) custom-call(f32[7,64,256]{2,1,0:T(8,128)S(1)} %collective-permute-done.before, f32[16,64,256]{2,1,0:T(8,128)S(1)} %copy-done, f32[7,64,256]{2,1,0:T(8,128)S(1)} %collective-permute-done.1.after, f32[2,16,64,256]{3,2,1,0:T(8,128)S(1)} %copy-done.1, ...), custom_call_target="tpu_custom_call" | custom-call | flops 3623878656 | bytes 4000000 | tf_op jit(solution)/shard_map/forward1/pallas_call | solution.py:257
  32.1 3.6 %collective-permute-start.2 = (f32[7,64,256]{2,1,0:T(8,128)S(1)}, f32[7,64,256]{2,1,0:T(8,128)S(1)}, u32[]{:S(2)}, u32[]{:S(2)}) collective-permute-start(f32[7,64,256]{2,1,0:T(8,128)S(1)} %get-tuple-element.20), channel_id=1, source_target_pairs={{0,4},{4,8},{8,12},{1,5},{5,9},{9,13},{2,6},{6,10},{10,14},{3,7},{... | collective-permute-start | bytes 1376264 | tf_op jit(solution)/shard_map/ppermute | solution.py:274
  35.8 2.1 %collective-permute-start.3 = (f32[7,64,256]{2,1,0:T(8,128)S(1)}, f32[7,64,256]{2,1,0:T(8,128)S(1)}, u32[]{:S(2)}, u32[]{:S(2)}) collective-permute-start(f32[7,64,256]{2,1,0:T(8,128)S(1)} %get-tuple-element.22), channel_id=1, source_target_pairs={{4,0},{8,4},{12,8},{5,1},{9,5},{13,9},{6,2},{10,6},{14,10},{7,3},{... | collective-permute-start | bytes 1376264 | tf_op jit(solution)/shard_map/ppermute | solution.py:274
  37.9 0.0 collective-permute-done.4.refs_0_
  37.9 0.0 collective-permute-done.5.refs_2_
  37.9 2.5 %back_early.1.refs_8_ = f32[8,64,256]{2,1,0:T(8,128)S(1)} custom-call(f32[7,64,256]{2,1,0:T(8,128)S(1)} %collective-permute-done.4.refs_0_, f32[16,64,256]{2,1,0:T(8,128)S(1)} %get-tuple-element.25.refs_1_, f32[7,64,256]{2,1,0:T(8,128)S(1)} %collective-permute-done.5.refs_2_, f32[2,16,64,256]{3,2,1,0:T(8,128)S(1)} %get-tuple-element.23.refs_3_.refs_11_, ...), custom_call_target="tpu_custom_call" | custom-call | flops 1811939328 | bytes 4000000 | tf_op jit(solution)/shard_map/back_early/pallas_call | solution.py:292
  40.4 0.8 collective-permute-done.2.refs_0_.refs_8_
  41.2 4.4 %collective-permute-done.3.refs_2_.refs_10_ = f32[7,64,256]{2,1,0:T(8,128)S(1)} collective-permute-done((f32[7,64,256]{2,1,0:T(8,128)S(1)}, f32[7,64,256]{2,1,0:T(8,128)S(1)}, u32[]{:S(2)}, u32[]{:S(2)}) %collective-permute-start.3) | collective-permute-done | bytes 458784 | tf_op jit(solution)/shard_map/ppermute | solution.py:274
  45.6 1.3 %back0.1.refs_9_ = f32[4,64,256]{2,1,0:T(8,128)S(1)} custom-call(f32[7,64,256]{2,1,0:T(8,128)S(1)} %collective-permute-done.2.refs_0_.refs_8_, f32[16,64,256]{2,1,0:T(8,128)S(1)} %get-tuple-element.21.refs_1_.refs_9_, f32[7,64,256]{2,1,0:T(8,128)S(1)} %collective-permute-done.3.refs_2_.refs_10_, f32[2,16,64,256]{3,2,1,0:T(8,128)S(1)} %get-tuple-element.23.refs_3_.refs_11_, ...), custom_call_target="tpu_custom_call" | custom-call | flops 905969664 | bytes 4000000 | tf_op jit(solution)/shard_map/back0/pallas_call | solution.py:292
  46.9 1.3 %back1.1.refs_16_ = f32[4,64,256]{2,1,0:T(8,128)S(1)} custom-call(f32[7,64,256]{2,1,0:T(8,128)S(1)} %collective-permute-done.2.refs_0_.refs_8_, f32[16,64,256]{2,1,0:T(8,128)S(1)} %get-tuple-element.21.refs_1_.refs_9_, f32[7,64,256]{2,1,0:T(8,128)S(1)} %collective-permute-done.3.refs_2_.refs_10_, f32[2,16,64,256]{3,2,1,0:T(8,128)S(1)} %get-tuple-element.23.refs_3_.refs_11_, ...), custom_call_target="tpu_custom_call" | custom-call | flops 905969664 | bytes 4000000 | tf_op jit(solution)/shard_map/back1/pallas_call | solution.py:292
  48.3 2.5 %back2.1.refs_16_ = f32[4,64,256]{2,1,0:T(8,128)S(1)} custom-call(f32[7,64,256]{2,1,0:T(8,128)S(1)} %collective-permute-done.4.refs_0_, f32[16,64,256]{2,1,0:T(8,128)S(1)} %get-tuple-element.25.refs_1_, f32[7,64,256]{2,1,0:T(8,128)S(1)} %collective-permute-done.5.refs_2_, f32[2,16,64,256]{3,2,1,0:T(8,128)S(1)} %get-tuple-element.23.refs_3_.refs_11_, ...), custom_call_target="tpu_custom_call" | custom-call | flops 1811939328 | bytes 4000000 | tf_op jit(solution)/shard_map/back2/pallas_call | solution.py:292
  50.8 2.5 %back3.1 = f32[4,64,256]{2,1,0:T(8,128)S(1)} custom-call(f32[7,64,256]{2,1,0:T(8,128)S(1)} %collective-permute-done.4.refs_0_, f32[16,64,256]{2,1,0:T(8,128)S(1)} %get-tuple-element.25.refs_1_, f32[7,64,256]{2,1,0:T(8,128)S(1)} %collective-permute-done.5.refs_2_, f32[2,16,64,256]{3,2,1,0:T(8,128)S(1)} %get-tuple-element.23.refs_3_.refs_11_, ...), custom_call_target="tpu_custom_call" | custom-call | flops 1811939328 | bytes 4000000 | tf_op jit(solution)/shard_map/back3/pallas_call | solution.py:292
  53.3 3.2 %collective-permute-start.15 = (f32[4,64,256]{2,1,0:T(8,128)S(1)}, f32[4,64,256]{2,1,0:T(8,128)S(1)}, u32[]{:S(2)}, u32[]{:S(2)}) collective-permute-start(f32[4,64,256]{2,1,0:T(8,128)S(1)} %back3.1), channel_id=1, source_target_pairs={{0,1},{3,2},{4,5},{7,6},{8,9},{11,10},{12,13},{15,14},{16,17},{19,... | collective-permute-start | bytes 786440 | tf_op jit(solution)/shard_map/ppermute | solution.py:329
  56.5 1.3 %collective-permute-start.12 = (f32[4,64,256]{2,1,0:T(8,128)S(1)}, f32[4,64,256]{2,1,0:T(8,128)S(1)}, u32[]{:S(2)}, u32[]{:S(2)}) collective-permute-start(f32[4,64,256]{2,1,0:T(8,128)S(1)} %back2.1.refs_16_), channel_id=1, source_target_pairs={{0,1},{3,2},{4,5},{7,6},{8,9},{11,10},{12,13},{15,14},{16,17},{19,... | collective-permute-start | bytes 786440 | tf_op jit(solution)/shard_map/ppermute | solution.py:329
  57.8 1.3 %collective-permute-start.9 = (f32[4,64,256]{2,1,0:T(8,128)S(1)}, f32[4,64,256]{2,1,0:T(8,128)S(1)}, u32[]{:S(2)}, u32[]{:S(2)}) collective-permute-start(f32[4,64,256]{2,1,0:T(8,128)S(1)} %back1.1.refs_16_), channel_id=1, source_target_pairs={{0,1},{3,2},{4,5},{7,6},{8,9},{11,10},{12,13},{15,14},{16,17},{19,... | collective-permute-start | bytes 786440 | tf_op jit(solution)/shard_map/ppermute | solution.py:329
  59.2 1.3 %collective-permute-start.6 = (f32[4,64,256]{2,1,0:T(8,128)S(1)}, f32[4,64,256]{2,1,0:T(8,128)S(1)}, u32[]{:S(2)}, u32[]{:S(2)}) collective-permute-start(f32[4,64,256]{2,1,0:T(8,128)S(1)} %back0.1.refs_9_), channel_id=1, source_target_pairs={{0,1},{3,2},{4,5},{7,6},{8,9},{11,10},{12,13},{15,14},{16,17},{19,... | collective-permute-start | bytes 786440 | tf_op jit(solution)/shard_map/ppermute | solution.py:329
  60.5 2.1 %collective-permute-done.15 = f32[4,64,256]{2,1,0:T(8,128)S(1)} collective-permute-done((f32[4,64,256]{2,1,0:T(8,128)S(1)}, f32[4,64,256]{2,1,0:T(8,128)S(1)}, u32[]{:S(2)}, u32[]{:S(2)}) %collective-permute-start.15) | collective-permute-done | bytes 262176 | tf_op jit(solution)/shard_map/ppermute | solution.py:329
  62.7 0.7 collective-permute-start.16
  63.3 4.9 %collective-permute-done.12 = f32[4,64,256]{2,1,0:T(8,128)S(1)} collective-permute-done((f32[4,64,256]{2,1,0:T(8,128)S(1)}, f32[4,64,256]{2,1,0:T(8,128)S(1)}, u32[]{:S(2)}, u32[]{:S(2)}) %collective-permute-start.12) | collective-permute-done | bytes 262176 | tf_op jit(solution)/shard_map/ppermute | solution.py:329
  68.3 0.7 collective-permute-start.13
  69.0 2.1 %collective-permute-done.9 = f32[4,64,256]{2,1,0:T(8,128)S(1)} collective-permute-done((f32[4,64,256]{2,1,0:T(8,128)S(1)}, f32[4,64,256]{2,1,0:T(8,128)S(1)}, u32[]{:S(2)}, u32[]{:S(2)}) %collective-permute-start.9) | collective-permute-done | bytes 262176 | tf_op jit(solution)/shard_map/ppermute | solution.py:329
  71.1 0.7 collective-permute-start.10
  71.8 2.1 %collective-permute-done.6 = f32[4,64,256]{2,1,0:T(8,128)S(1)} collective-permute-done((f32[4,64,256]{2,1,0:T(8,128)S(1)}, f32[4,64,256]{2,1,0:T(8,128)S(1)}, u32[]{:S(2)}, u32[]{:S(2)}) %collective-permute-start.6) | collective-permute-done | bytes 262176 | tf_op jit(solution)/shard_map/ppermute | solution.py:329
  73.9 0.7 collective-permute-start.7
  74.6 0.0 collective-permute-done.16
  74.6 1.3 %collective-permute-start.17 = (f32[4,64,256]{2,1,0:T(8,128)S(1)}, f32[4,64,256]{2,1,0:T(8,128)S(1)}, u32[]{:S(2)}, u32[]{:S(2)}) collective-permute-start(f32[4,64,256]{2,1,0:T(8,128)S(1)} %add.31), channel_id=1, source_target_pairs={{1,0},{2,3},{5,4},{6,7},{9,8},{10,11},{13,12},{14,15},{17,16},{18,... | collective-permute-start | bytes 786440 | tf_op jit(solution)/shard_map/ppermute | solution.py:333
  75.9 0.0 collective-permute-done.13
  76.0 1.3 %collective-permute-start.14 = (f32[4,64,256]{2,1,0:T(8,128)S(1)}, f32[4,64,256]{2,1,0:T(8,128)S(1)}, u32[]{:S(2)}, u32[]{:S(2)}) collective-permute-start(f32[4,64,256]{2,1,0:T(8,128)S(1)} %add.29), channel_id=1, source_target_pairs={{1,0},{2,3},{5,4},{6,7},{9,8},{10,11},{13,12},{14,15},{17,16},{18,... | collective-permute-start | bytes 786440 | tf_op jit(solution)/shard_map/ppermute | solution.py:333
  77.3 0.0 collective-permute-done.10
  77.4 1.3 %collective-permute-start.11 = (f32[4,64,256]{2,1,0:T(8,128)S(1)}, f32[4,64,256]{2,1,0:T(8,128)S(1)}, u32[]{:S(2)}, u32[]{:S(2)}) collective-permute-start(f32[4,64,256]{2,1,0:T(8,128)S(1)} %add.27), channel_id=1, source_target_pairs={{1,0},{2,3},{5,4},{6,7},{9,8},{10,11},{13,12},{14,15},{17,16},{18,... | collective-permute-start | bytes 786440 | tf_op jit(solution)/shard_map/ppermute | solution.py:333
  78.7 0.0 collective-permute-done.7
  78.7 1.3 %collective-permute-start.8 = (f32[4,64,256]{2,1,0:T(8,128)S(1)}, f32[4,64,256]{2,1,0:T(8,128)S(1)}, u32[]{:S(2)}, u32[]{:S(2)}) collective-permute-start(f32[4,64,256]{2,1,0:T(8,128)S(1)} %add.25), channel_id=1, source_target_pairs={{1,0},{2,3},{5,4},{6,7},{9,8},{10,11},{13,12},{14,15},{17,16},{18,... | collective-permute-start | bytes 786440 | tf_op jit(solution)/shard_map/ppermute | solution.py:333
  80.0 7.5 %collective-permute-done.17 = f32[4,64,256]{2,1,0:T(8,128)S(1)} collective-permute-done((f32[4,64,256]{2,1,0:T(8,128)S(1)}, f32[4,64,256]{2,1,0:T(8,128)S(1)}, u32[]{:S(2)}, u32[]{:S(2)}) %collective-permute-start.17) | collective-permute-done | bytes 262176 | tf_op jit(solution)/shard_map/ppermute | solution.py:333
  87.5 5.6 %collective-permute-done.14 = f32[4,64,256]{2,1,0:T(8,128)S(1)} collective-permute-done((f32[4,64,256]{2,1,0:T(8,128)S(1)}, f32[4,64,256]{2,1,0:T(8,128)S(1)}, u32[]{:S(2)}, u32[]{:S(2)}) %collective-permute-start.14) | collective-permute-done | bytes 262176 | tf_op jit(solution)/shard_map/ppermute | solution.py:333
  93.2 3.3 %collective-permute-done.11 = f32[4,64,256]{2,1,0:T(8,128)S(1)} collective-permute-done((f32[4,64,256]{2,1,0:T(8,128)S(1)}, f32[4,64,256]{2,1,0:T(8,128)S(1)}, u32[]{:S(2)}, u32[]{:S(2)}) %collective-permute-start.11) | collective-permute-done | bytes 262176 | tf_op jit(solution)/shard_map/ppermute | solution.py:333
  96.5 2.8 %collective-permute-done.8 = f32[4,64,256]{2,1,0:T(8,128)S(1)} collective-permute-done((f32[4,64,256]{2,1,0:T(8,128)S(1)}, f32[4,64,256]{2,1,0:T(8,128)S(1)}, u32[]{:S(2)}, u32[]{:S(2)}) %collective-permute-start.8) | collective-permute-done | bytes 262176 | tf_op jit(solution)/shard_map/ppermute | solution.py:333
  99.3 1.0 %pad_maximum_fusion = f32[16,64,256]{2,1,0:T(8,128)} fusion(f32[4,64,256]{2,1,0:T(8,128)S(1)} %broadcast_select_fusion, f32[4,64,256]{2,1,0:T(8,128)S(1)} %broadcast_select_fusion.1, f32[4,64,256]{2,1,0:T(8,128)S(1)} %broadcast_select_fusion.2, f32[4,64,256]{2,1,0:T(8,128)S(1)} %broadcast_select_fusion.3), kind=kLoop, calls=%fused_computation | loop fusion | flops 786432 | bytes 2097152 | tf_op jit(solution)/shard_map/concatenate | solution.py:317
  (12 shorter events, 0.4 us)
Async XLA Ops:
  1.2 13.9 %collective-permute-start = (f32[7,64,256]{2,1,0:T(8,128)S(1)}, f32[7,64,256]{2,1,0:T(8,128)S(1)}, u32[]{:S(2)}, u32[]{:S(2)}) collective-permute-start(f32[7,64,256]{2,1,0:T(8,128)S(1)} %get-tuple-element.28), channel_id=1, source_target_pairs={{0,4},{4,8},{8,12},{1,5},{5,9},{9,13},{2,6},{6,10},{10,14},{3,7},{... | collective-permute-start | bytes 1376264 | tf_op jit(solution)/shard_map/ppermute | solution.py:226
  5.8 9.8 %collective-permute-start.1 = (f32[7,64,256]{2,1,0:T(8,128)S(1)}, f32[7,64,256]{2,1,0:T(8,128)S(1)}, u32[]{:S(2)}, u32[]{:S(2)}) collective-permute-start(f32[7,64,256]{2,1,0:T(8,128)S(1)} %get-tuple-element.27), channel_id=1, source_target_pairs={{4,0},{8,4},{12,8},{5,1},{9,5},{13,9},{6,2},{10,6},{14,10},{7,3},{... | collective-permute-start | bytes 1376264 | tf_op jit(solution)/shard_map/ppermute | solution.py:227
  7.7 1.2 %copy-start = (f32[16,64,256]{2,1,0:T(8,128)S(1)}, f32[16,64,256]{2,1,0:T(8,128)}, u32[]{:S(2)}) copy-start(f32[16,64,256]{2,1,0:T(8,128)} %est.5) | copy-start | bytes 3145732
  8.9 0.7 copy-start.2
  9.6 0.7 copy-start.3
  10.3 0.7 copy-start.4
  11.0 0.7 copy-start.5
  11.6 0.7 copy-start.6
  12.3 3.3 %copy-start.1 = (f32[2,16,64,256]{3,2,1,0:T(8,128)S(1)}, f32[2,16,64,256]{3,2,1,0:T(8,128)}, u32[]{:S(2)}) copy-start(f32[2,16,64,256]{3,2,1,0:T(8,128)} %measured.3) | copy-start | bytes 6291460
  21.2 16.7 %collective-permute-start.4 = (f32[7,64,256]{2,1,0:T(8,128)S(1)}, f32[7,64,256]{2,1,0:T(8,128)S(1)}, u32[]{:S(2)}, u32[]{:S(2)}) collective-permute-start(f32[7,64,256]{2,1,0:T(8,128)S(1)} %get-tuple-element.24), channel_id=1, source_target_pairs={{0,4},{4,8},{8,12},{1,5},{5,9},{9,13},{2,6},{6,10},{10,14},{3,7},{... | collective-permute-start | bytes 1376264 | tf_op jit(solution)/shard_map/ppermute | solution.py:274
  24.5 13.4 %collective-permute-start.5 = (f32[7,64,256]{2,1,0:T(8,128)S(1)}, f32[7,64,256]{2,1,0:T(8,128)S(1)}, u32[]{:S(2)}, u32[]{:S(2)}) collective-permute-start(f32[7,64,256]{2,1,0:T(8,128)S(1)} %get-tuple-element.26), channel_id=1, source_target_pairs={{4,0},{8,4},{12,8},{5,1},{9,5},{13,9},{6,2},{10,6},{14,10},{7,3},{... | collective-permute-start | bytes 1376264 | tf_op jit(solution)/shard_map/ppermute | solution.py:274
  32.1 9.0 %collective-permute-start.2 = (f32[7,64,256]{2,1,0:T(8,128)S(1)}, f32[7,64,256]{2,1,0:T(8,128)S(1)}, u32[]{:S(2)}, u32[]{:S(2)}) collective-permute-start(f32[7,64,256]{2,1,0:T(8,128)S(1)} %get-tuple-element.20), channel_id=1, source_target_pairs={{0,4},{4,8},{8,12},{1,5},{5,9},{9,13},{2,6},{6,10},{10,14},{3,7},{... | collective-permute-start | bytes 1376264 | tf_op jit(solution)/shard_map/ppermute | solution.py:274
  35.8 9.8 %collective-permute-start.3 = (f32[7,64,256]{2,1,0:T(8,128)S(1)}, f32[7,64,256]{2,1,0:T(8,128)S(1)}, u32[]{:S(2)}, u32[]{:S(2)}) collective-permute-start(f32[7,64,256]{2,1,0:T(8,128)S(1)} %get-tuple-element.22), channel_id=1, source_target_pairs={{4,0},{8,4},{12,8},{5,1},{9,5},{13,9},{6,2},{10,6},{14,10},{7,3},{... | collective-permute-start | bytes 1376264 | tf_op jit(solution)/shard_map/ppermute | solution.py:274
  53.3 9.3 %collective-permute-start.15 = (f32[4,64,256]{2,1,0:T(8,128)S(1)}, f32[4,64,256]{2,1,0:T(8,128)S(1)}, u32[]{:S(2)}, u32[]{:S(2)}) collective-permute-start(f32[4,64,256]{2,1,0:T(8,128)S(1)} %back3.1), channel_id=1, source_target_pairs={{0,1},{3,2},{4,5},{7,6},{8,9},{11,10},{12,13},{15,14},{16,17},{19,... | collective-permute-start | bytes 786440 | tf_op jit(solution)/shard_map/ppermute | solution.py:329
  56.5 11.7 %collective-permute-start.12 = (f32[4,64,256]{2,1,0:T(8,128)S(1)}, f32[4,64,256]{2,1,0:T(8,128)S(1)}, u32[]{:S(2)}, u32[]{:S(2)}) collective-permute-start(f32[4,64,256]{2,1,0:T(8,128)S(1)} %back2.1.refs_16_), channel_id=1, source_target_pairs={{0,1},{3,2},{4,5},{7,6},{8,9},{11,10},{12,13},{15,14},{16,17},{19,... | collective-permute-start | bytes 786440 | tf_op jit(solution)/shard_map/ppermute | solution.py:329
  57.8 13.2 %collective-permute-start.9 = (f32[4,64,256]{2,1,0:T(8,128)S(1)}, f32[4,64,256]{2,1,0:T(8,128)S(1)}, u32[]{:S(2)}, u32[]{:S(2)}) collective-permute-start(f32[4,64,256]{2,1,0:T(8,128)S(1)} %back1.1.refs_16_), channel_id=1, source_target_pairs={{0,1},{3,2},{4,5},{7,6},{8,9},{11,10},{12,13},{15,14},{16,17},{19,... | collective-permute-start | bytes 786440 | tf_op jit(solution)/shard_map/ppermute | solution.py:329
  59.2 14.7 %collective-permute-start.6 = (f32[4,64,256]{2,1,0:T(8,128)S(1)}, f32[4,64,256]{2,1,0:T(8,128)S(1)}, u32[]{:S(2)}, u32[]{:S(2)}) collective-permute-start(f32[4,64,256]{2,1,0:T(8,128)S(1)} %back0.1.refs_9_), channel_id=1, source_target_pairs={{0,1},{3,2},{4,5},{7,6},{8,9},{11,10},{12,13},{15,14},{16,17},{19,... | collective-permute-start | bytes 786440 | tf_op jit(solution)/shard_map/ppermute | solution.py:329
  62.7 11.9 %collective-permute-start.16 = (f32[4,64,256]{2,1,0:T(8,128)S(1)}, f32[4,64,256]{2,1,0:T(8,128)S(1)}, u32[]{:S(2)}, u32[]{:S(2)}) collective-permute-start(f32[4,64,256]{2,1,0:T(8,128)S(1)} %add.30), channel_id=1, source_target_pairs={{1,2},{2,1},{5,6},{6,5},{9,10},{10,9},{13,14},{14,13},{17,18},{18,... | collective-permute-start | bytes 786440 | tf_op jit(solution)/shard_map/ppermute | solution.py:330
  68.3 7.7 %collective-permute-start.13 = (f32[4,64,256]{2,1,0:T(8,128)S(1)}, f32[4,64,256]{2,1,0:T(8,128)S(1)}, u32[]{:S(2)}, u32[]{:S(2)}) collective-permute-start(f32[4,64,256]{2,1,0:T(8,128)S(1)} %add.28), channel_id=1, source_target_pairs={{1,2},{2,1},{5,6},{6,5},{9,10},{10,9},{13,14},{14,13},{17,18},{18,... | collective-permute-start | bytes 786440 | tf_op jit(solution)/shard_map/ppermute | solution.py:330
  71.1 6.2 %collective-permute-start.10 = (f32[4,64,256]{2,1,0:T(8,128)S(1)}, f32[4,64,256]{2,1,0:T(8,128)S(1)}, u32[]{:S(2)}, u32[]{:S(2)}) collective-permute-start(f32[4,64,256]{2,1,0:T(8,128)S(1)} %add.26), channel_id=1, source_target_pairs={{1,2},{2,1},{5,6},{6,5},{9,10},{10,9},{13,14},{14,13},{17,18},{18,... | collective-permute-start | bytes 786440 | tf_op jit(solution)/shard_map/ppermute | solution.py:330
  73.9 4.8 %collective-permute-start.7 = (f32[4,64,256]{2,1,0:T(8,128)S(1)}, f32[4,64,256]{2,1,0:T(8,128)S(1)}, u32[]{:S(2)}, u32[]{:S(2)}) collective-permute-start(f32[4,64,256]{2,1,0:T(8,128)S(1)} %add.24), channel_id=1, source_target_pairs={{1,2},{2,1},{5,6},{6,5},{9,10},{10,9},{13,14},{14,13},{17,18},{18,... | collective-permute-start | bytes 786440 | tf_op jit(solution)/shard_map/ppermute | solution.py:330
  74.6 12.9 %collective-permute-start.17 = (f32[4,64,256]{2,1,0:T(8,128)S(1)}, f32[4,64,256]{2,1,0:T(8,128)S(1)}, u32[]{:S(2)}, u32[]{:S(2)}) collective-permute-start(f32[4,64,256]{2,1,0:T(8,128)S(1)} %add.31), channel_id=1, source_target_pairs={{1,0},{2,3},{5,4},{6,7},{9,8},{10,11},{13,12},{14,15},{17,16},{18,... | collective-permute-start | bytes 786440 | tf_op jit(solution)/shard_map/ppermute | solution.py:333
  76.0 17.1 %collective-permute-start.14 = (f32[4,64,256]{2,1,0:T(8,128)S(1)}, f32[4,64,256]{2,1,0:T(8,128)S(1)}, u32[]{:S(2)}, u32[]{:S(2)}) collective-permute-start(f32[4,64,256]{2,1,0:T(8,128)S(1)} %add.29), channel_id=1, source_target_pairs={{1,0},{2,3},{5,4},{6,7},{9,8},{10,11},{13,12},{14,15},{17,16},{18,... | collective-permute-start | bytes 786440 | tf_op jit(solution)/shard_map/ppermute | solution.py:333
  77.4 19.1 %collective-permute-start.11 = (f32[4,64,256]{2,1,0:T(8,128)S(1)}, f32[4,64,256]{2,1,0:T(8,128)S(1)}, u32[]{:S(2)}, u32[]{:S(2)}) collective-permute-start(f32[4,64,256]{2,1,0:T(8,128)S(1)} %add.27), channel_id=1, source_target_pairs={{1,0},{2,3},{5,4},{6,7},{9,8},{10,11},{13,12},{14,15},{17,16},{18,... | collective-permute-start | bytes 786440 | tf_op jit(solution)/shard_map/ppermute | solution.py:333
  78.7 20.6 %collective-permute-start.8 = (f32[4,64,256]{2,1,0:T(8,128)S(1)}, f32[4,64,256]{2,1,0:T(8,128)S(1)}, u32[]{:S(2)}, u32[]{:S(2)}) collective-permute-start(f32[4,64,256]{2,1,0:T(8,128)S(1)} %add.25), channel_id=1, source_target_pairs={{1,0},{2,3},{5,4},{6,7},{9,8},{10,11},{13,12},{14,15},{17,16},{18,... | collective-permute-start | bytes 786440 | tf_op jit(solution)/shard_map/ppermute | solution.py:333
where the time goes:
time: 101 us; the launch traced here: 100 us
  waiting for transfers between devices  36 us (36%)
  starting transfers between devices  32.4 us (32%)
  Pallas kernels  24.4 us (24%)
  local copies, waits for them, and re-layouts  5.81 us (6%)
  other arithmetic  1.46 us (1%)
    ppermute x4, waiting for transfers between devices, summed_over(): moved = lax.ppermute(piece, axis, [(low + 1, low), (high - 1, high)])  19.2 us
    pallas_call x2, Pallas kernels, per_device(): pl.pallas_call(functools.partial(forward_kernel, chunk, reach), grid=(chu...  11.3 us
    ppermute x4, waiting for transfers between devices, summed_over(): lax.ppermute(piece, axis, [(s, s + 1), (count - 1 - s, count - 2 - s)])  11.2 us
    pallas_call x5, Pallas kernels, backward(): pl.pallas_call(functools.partial(backward_kernel, chunk, reach, first, co...  10.2 us
    ppermute x4, starting transfers between devices, summed_over(): lax.ppermute(piece, axis, [(s, s + 1), (count - 1 - s, count - 2 - s)])  7.13 us
    ppermute x2, starting transfers between devices, per_device(): lax.ppermute(tail, 'slab', up)  6.93 us
    ppermute x4, starting transfers between devices, summed_over(): moved = lax.ppermute(piece, axis, [(low + 1, low), (high - 1, high)])  5.17 us
    unnamed x14, local copies, waits for them, and re-layouts  4.59 us
  transfers between devices with their start and end apart: 18, of which 11 were waited for; matrix products, arithmetic and copies ran while one was open for 0% of the time, Pallas kernels for 11%

commit v1 on v0

--- a/solution.py
+++ b/solution.py
@@ -7,10 +7,11 @@
 from jax.experimental.pallas import tpu as pltpu
 from jax.sharding import PartitionSpec as P
 
+
 f32 = jnp.float32
 bf16 = jnp.bfloat16
 SUB = 8
-VMEM_LIMIT = 24 * 2**20
+VMEM_LIMIT = 13 * 2**20
 
 
 def split(values):
@@ -38,7 +39,14 @@
     return row
 
 
-def prep_kernel(chunk, psf_z, psf_y, psf_x, table, index, est, xh, xl, ym, zm, scale):
+def prep_kernel(chunk, *refs):
+    far, (est, xh, xl, ym, zm, scale), near, done = refs[:5], refs[5:11], refs[11:16], refs[16]
+    copies = [pltpu.make_async_copy(a, b, done.at[i]) for i, (a, b) in enumerate(zip(far, near))]
+    for copy in copies:
+        copy.start()
+    for copy in copies:
+        copy.wait()
+    psf_z, psf_y, psf_x, table, index = near
     members, rank, taps = psf_x.shape
     planes, height, width = est.shape
     radius = (taps - 1) // 2
@@ -106,16 +114,26 @@
             scale[m, z] = est[z] * (weight / (grand * normal))
 
 
-def load_split(pieces, first, last, high, low):
-    starts = [0]
-    for piece in pieces:
-        starts.append(starts[-1] + piece.shape[0])
+def load_split(own, got, first, last, high, low):
+    radius, planes = got[0].shape[0], own.shape[0]
+    slab, slabs = lax.axis_index("slab"), lax.axis_size("slab")
+    even = lax.rem(slab, 2) == 0
+
+    def before(a, b, rows):
+        piece = jnp.where(even, got[1][a:b, rows, :], got[0][a:b, rows, :])
+        return jnp.where(slab > 0, piece, 0.0)
+
+    def after(a, b, rows):
+        piece = jnp.where(even, got[0][a:b, rows, :], got[1][a:b, rows, :])
+        return jnp.where(slab < slabs - 1, piece, 0.0)
+
+    sources = [(0, radius, before), (radius, planes, lambda a, b, rows: own[a:b, rows, :]), (radius + planes, radius, after)]
     for block in range(high.shape[0]):
         parts = []
-        for piece, start in zip(pieces, starts):
-            a, b = max(first - start, 0), min(last - start, piece.shape[0])
+        for start, count, read in sources:
+            a, b = max(first - start, 0), min(last - start, count)
             if a < b:
-                parts.append(piece[a:b, block * SUB : (block + 1) * SUB, :])
+                parts.append(read(a, b, slice(block * SUB, (block + 1) * SUB)))
         rows = jnp.concatenate(parts, axis=0)
         rows = rows.reshape((last - first) * SUB, rows.shape[2])
         h, l = split(rows)
@@ -154,14 +172,14 @@
     return results
 
 
-def forward_kernel(chunk, reach, before, est, after, measured, *rest):
-    mats, (ratio, head, tail, high, low, *scratch) = rest[:4], rest[4:]
+def forward_kernel(chunk, reach, est, got_a, got_b, measured, *rest):
+    mats, (ratio, send_a, send_b, high, low, *scratch) = rest[:4], rest[4:]
     c = pl.program_id(0)
-    planes = ratio.shape[0]
+    planes, radius = ratio.shape[0], send_a.shape[0]
 
     @pl.when(c == 0)
     def _():
-        load_split((before, est, after), 0, planes + reach, high, low)
+        load_split(est, (got_a, got_b), 0, planes + reach, high, low)
 
     blurred = apply_chunk(c, chunk, reach, high, low, mats, scratch)
     for z in range(chunk):
@@ -169,8 +187,10 @@
 
     @pl.when(c == pl.num_programs(0) - 1)
     def _():
-        head[...] = ratio[0 : head.shape[0]]
-        tail[...] = ratio[planes - tail.shape[0] : planes]
+        even = lax.rem(lax.axis_index("slab"), 2) == 0
+        head, tail = ratio[0:radius], ratio[planes - radius : planes]
+        send_a[...] = jnp.where(even, tail, head)
+        send_b[...] = jnp.where(even, head, tail)
 
 
 def backward_kernel(chunk, reach, first, count, views, has_sum, has_after, *refs):
@@ -180,19 +200,28 @@
     running = take(1)[0] if has_sum else None
     if has_after:
         take(1)
-    (out,) = take(1)
+    outs = take(len(refs) - 5)
     high, low, *scratch = refs
+    step = outs[0].shape[0]
     for i, (pieces, scale, mats) in enumerate(per_view):
-        load_split(pieces, first * chunk, (first + count) * chunk + reach, high, low)
+        load_split(pieces[0], pieces[1:], first * chunk, (first + count) * chunk + reach, high, low)
         for c in range(count):
             back = apply_chunk(c, chunk, reach, high, low, mats, scratch)
             for z in range(chunk):
-                term = back[z] * scale[c * chunk + z]
+                place = c * chunk + z
+                out = outs[place // step]
+                term = back[z] * scale[place]
                 if i:
-                    term = term + out[c * chunk + z]
+                    term = term + out[place % step]
                 elif has_sum:
-                    term = term + running[z]
-                out[c * chunk + z] = term
+                    term = term + running[place]
+                out[place % step] = term
+
+
+def finish_kernel(got, own, *rest):
+    place, count = lax.axis_index("view"), lax.axis_size("view")
+    end = (place == 0) | (place == count - 1)
+    rest[-1][...] = jnp.where(end, got[...], own[...])
 
 
 def whole(shape):
@@ -213,18 +242,26 @@
     struct = jax.ShapeDtypeStruct
     plane = (height, width)
     params = pltpu.CompilerParams(vmem_limit_bytes=VMEM_LIMIT)
-    smem = pl.BlockSpec(memory_space=pltpu.SMEM)
-
-    slabs = lax.axis_size("slab")
-    up = [(i, i + 1) for i in range(slabs - 1)]
-    down = [(i + 1, i) for i in range(slabs - 1)]
+    small = [pltpu.with_memory_space_constraint(a, pltpu.HBM) for a in (psf_z, psf_y, psf_x, weight_table, weight_index)]
 
     def cost(fraction):
         flops = 2 * 6912 * 65536 * chunks * fraction
         return pl.CostEstimate(flops=int(flops), bytes_accessed=int(4e6), transcendentals=0)
 
-    before = lax.ppermute(estimate[planes - radius :], "slab", up)
-    after = lax.ppermute(estimate[:radius], "slab", down)
+    slabs, line = lax.axis_size("slab"), lax.axis_size("view")
+    even = lax.rem(lax.axis_index("slab"), 2) == 0
+    across = [swaps(slabs, line, 0, 0), swaps(slabs, line, 0, 1)]
+    along = [swaps(slabs, line, 1, 0), swaps(slabs, line, 1, 1)]
+
+    def exchange(send, perm, name):
+        with jax.named_scope(name):
+            return lax.ppermute(send, ("slab", "view"), perm)
+
+    head, tail = estimate[:radius], estimate[planes - radius :]
+    got = [
+        exchange(jnp.where(even, tail, head), across[0], "est_a"),
+        exchange(jnp.where(even, head, tail), across[1], "est_b"),
+    ]
     depth_lanes = -(-(chunk + reach) * SUB // 128) * 128
     slots = 2 * members
     mats_and_scale = pl.pallas_call(
@@ -236,11 +273,12 @@
             struct((slots, 2 * rank * chunk * SUB, depth_lanes), bf16),
             struct((members, planes) + plane, f32),
         ],
-        in_specs=[smem] * 5 + [pl.BlockSpec(memory_space=pltpu.VMEM)],
+        in_specs=[pl.BlockSpec(memory_space=pltpu.HBM)] * 5 + [pl.BlockSpec(memory_space=pltpu.VMEM)],
+        scratch_shapes=[pltpu.SMEM(a.shape, a.dtype) for a in small] + [pltpu.SemaphoreType.DMA((len(small),))],
         compiler_params=params,
         cost_estimate=cost(0.7),
         name="prep",
-    )(psf_z, psf_y, psf_x, weight_table, weight_index, estimate)
+    )(*small, estimate)
     mats, scale = mats_and_scale[:4], mats_and_scale[4]
 
     def work(window):
@@ -254,26 +292,29 @@
 
     extended = []
     for m in range(members):
-        ratio, head, tail = pl.pallas_call(
-            functools.partial(forward_kernel, chunk, reach),
-            grid=(chunks,),
-            out_shape=[struct((planes,) + plane, f32), struct((radius,) + plane, f32), struct((radius,) + plane, f32)],
-            in_specs=[
-                whole(before.shape),
-                whole(estimate.shape),
-                whole(after.shape),
-                pl.BlockSpec((None, chunk) + plane, lambda c, m=m: (m, c, 0, 0)),
-            ]
-            + [slot_of(a, 2 * m) for a in mats],
-            out_specs=[whole((planes,) + plane), whole((radius,) + plane), whole((radius,) + plane)],
-            scratch_shapes=work(planes + reach),
-            compiler_params=params,
-            cost_estimate=cost(1),
-            name=f"forward{m}",
-        )(before, estimate, after, measured, *mats)
-        extended.append((lax.ppermute(tail, "slab", up), ratio, lax.ppermute(head, "slab", down)))
-
-    def backward(views, first, count, running, after, name):
+        with jax.named_scope(f"fwd{m}"):
+            ratio, send_a, send_b = pl.pallas_call(
+                functools.partial(forward_kernel, chunk, reach),
+                grid=(chunks,),
+                out_shape=[struct((planes,) + plane, f32), struct((radius,) + plane, f32), struct((radius,) + plane, f32)],
+                in_specs=[
+                    whole(estimate.shape),
+                    whole(got[0].shape),
+                    whole(got[1].shape),
+                    pl.BlockSpec((None, chunk) + plane, lambda c, m=m: (m, c, 0, 0)),
+                ]
+                + [slot_of(a, 2 * m) for a in mats],
+                out_specs=[whole((planes,) + plane), whole((radius,) + plane), whole((radius,) + plane)],
+                scratch_shapes=work(planes + reach),
+                compiler_params=params,
+                cost_estimate=cost(1),
+                name=f"forward{m}",
+            )(estimate, *got, measured, *mats)
+        extended.append(
+            (ratio, exchange(send_a, across[0], f"ratio{m}_a"), exchange(send_b, across[1], f"ratio{m}_b"))
+        )
+
+    def backward(views, first, count, running, after, piece, name):
         operands, specs = [], []
         for m in views:
             operands += list(extended[m]) + [scale] + list(mats)
@@ -285,54 +326,110 @@
         if running is not None:
             source, place = running
             operands.append(source)
-            specs.append(pl.BlockSpec((chunk,) + plane, lambda *_: (place, 0, 0)))
+            specs.append(pl.BlockSpec((count * chunk,) + plane, lambda *_: (place // count, 0, 0)))
         if after is not None:
             operands.append(after)
-            specs.append(pl.BlockSpec(memory_space=pl.ANY))
-        return pl.pallas_call(
-            functools.partial(backward_kernel, chunk, reach, first, count, len(views), running is not None, after is not None),
-            grid=(1,),
-            out_shape=struct((count * chunk,) + plane, f32),
-            in_specs=specs,
-            out_specs=whole((count * chunk,) + plane),
-            scratch_shapes=work(count * chunk + reach),
-            compiler_params=params,
-            cost_estimate=cost(len(views) * count / chunks),
-            name=name,
-        )(*operands)
-
-    early = min(2, chunks) if members > 1 else 0
+            specs.append(pl.BlockSpec(memory_space=pltpu.HBM))
+        shapes = [(piece,) + plane] * (count * chunk // piece)
+        with jax.named_scope(name):
+            return pl.pallas_call(
+                functools.partial(backward_kernel, chunk, reach, first, count, len(views), running is not None, after is not None),
+                grid=(1,),
+                out_shape=[struct(shape, f32) for shape in shapes],
+                in_specs=specs,
+                out_specs=[whole(shape) for shape in shapes],
+                scratch_shapes=work(count * chunk + reach),
+                compiler_params=params,
+                cost_estimate=cost(len(views) * count / chunks),
+                name=name,
+            )(*operands)
+
     every = list(range(members))
-    previous = None
-    if early:
-        previous = partial = backward(every[:-1], 0, early, None, None, "back_early")
+    previous = partial = None
+    if members > 1:
+        (partial,) = backward(every[:-1], 0, chunks, None, None, planes, "early")
+        previous = partial
+    small_piece = max(chunk // 2, 1)
     pieces = []
     for c in range(chunks):
-        if c < early:
-            previous = backward(every[-1:], c, 1, (partial, c), previous if c else None, f"back{c}")
-        else:
-            previous = backward(every, c, 1, None, previous, f"back{c}")
-        pieces.append(previous)
-
-    return jnp.concatenate([summed_over(piece, "view") for piece in pieces], axis=0)
-
-
-def summed_over(piece, axis):
-    count = lax.axis_size(axis)
+        pieces += backward(
+            every[-1:], c, 1, None if partial is None else (partial, c), previous if c else None, small_piece, f"back{c}"
+        )
+        previous = pieces[-1]
+    return line_sum(pieces, along, exchange, (planes,) + plane)
+
+
+LAG = 3
+
+
+def line_sum(pieces, along, exchange, shape):
+    count = lax.axis_size("view")
+    sizes = [piece.shape[0] for piece in pieces]
     if count == 1:
-        return piece
+        return jnp.concatenate(pieces, axis=0)
     if count % 2:
-        return lax.psum(piece, axis)
+        return lax.psum(jnp.concatenate(pieces, axis=0), "view")
     half = count // 2
-    place = lax.axis_index(axis)
-    for s in range(half - 1):
-        piece = piece + lax.ppermute(piece, axis, [(s, s + 1), (count - 1 - s, count - 2 - s)])
-    piece = piece + lax.ppermute(piece, axis, [(half - 1, half), (half, half - 1)])
-    for s in range(half - 1):
-        low, high = half - 2 - s, half + 1 + s
-        moved = lax.ppermute(piece, axis, [(low + 1, low), (high - 1, high)])
-        piece = jnp.where((place == low) | (place == high), moved, piece)
-    return piece
+    last = 2 * half - 2
+    place = lax.axis_index("view")
+    depth = jnp.minimum(place, count - 1 - place)
+    pieces = list(pieces)
+    total = len(pieces)
+    out = None
+    for j in range(total + (last // 2) * LAG):
+        for odd in range(2):
+            live = [(j - (i // 2) * LAG, i) for i in range(odd, last + 1, 2)]
+            live = [(k, i) for k, i in live if 0 <= k < total]
+            if not live:
+                continue
+            send = pieces[live[0][0]]
+            for k, i in live[1:]:
+                sender = i if i < half else 2 * half - 1 - i
+                send = jnp.where(depth == sender, pieces[k], send)
+            got = exchange(send, along[odd], f"{'mid' if odd else 'out'}{j}x")
+            for k, i in live:
+                if i < half:
+                    target = min(i + 1, half - 1)
+                    pieces[k] = jnp.where(depth == target, pieces[k] + got, pieces[k])
+                elif i < last:
+                    pieces[k] = jnp.where(depth == last - i, got, pieces[k])
+                if i == last:
+                    out = finish(got if half > 1 else pieces[k], pieces[k], out, k, shape)
+    return out
+
+
+def finish(got, own, out, k, shape):
+    block = pl.BlockSpec(own.shape, lambda *_: (k, 0, 0))
+    with jax.named_scope(f"finish{k}x"):
+        return pl.pallas_call(
+            finish_kernel,
+            grid=(1,),
+            out_shape=jax.ShapeDtypeStruct(shape, f32),
+            in_specs=[whole(got.shape), whole(own.shape)] + ([pl.BlockSpec(memory_space=pltpu.HBM)] if out is not None else []),
+            out_specs=block,
+            input_output_aliases={2: 0} if out is not None else {},
+            compiler_params=pltpu.CompilerParams(vmem_limit_bytes=2**22),
+            cost_estimate=pl.CostEstimate(flops=1000, bytes_accessed=12 * own.size, transcendentals=0),
+            name=f"finish{k}",
+        )(got, own, *([] if out is None else [out]))
+
+
+def swaps(slabs, line, axis, odd):
+    pairs = []
+    for s in range(slabs):
+        for v in range(line):
+            here, sizes = [s, v], (slabs, line)
+            there = list(here)
+            step = 1 if (here[axis] - odd) % 2 == 0 else -1
+            if 0 <= here[axis] + step < sizes[axis]:
+                there[axis] += step
+            else:
+                other = 1 - axis
+                step = 1 if here[other] % 2 == 0 else -1
+                if 0 <= here[other] + step < sizes[other]:
+                    there[other] += step
+            pairs.append((s * line + v, there[0] * line + there[1]))
+    return pairs
 
 
 def solution(mesh):

time: 101 us -> 91.9 us (0.910)
  the two profiles are of different devices: /device:TPU:1 before, /device:TPU:0 now
where the time goes in v1:
time: 91.9 us; the launch traced here: 91.4 us
  Pallas kernels  37.8 us (41%)
  starting transfers between devices  33 us (36%)
  waiting for transfers between devices  11.1 us (12%)
  local copies, waits for them, and re-layouts  7.66 us (8%)
  other arithmetic  1.59 us (2%)
    ppermute x25, starting transfers between devices, exchange(): return lax.ppermute(send, ('slab', 'view'), perm)  33 us
    pallas_call x5, Pallas kernels, backward(): pl.pallas_call(functools.partial(backward_kernel, chunk, reach, first, co...  15.8 us
    pallas_call x2, Pallas kernels, per_device(): pl.pallas_call(functools.partial(forward_kernel, chunk, reach), grid=(chu...  13.4 us
    ppermute x25, waiting for transfers between devices, exchange(): return lax.ppermute(send, ('slab', 'view'), perm)  11.1 us
    unnamed x20, local copies, waits for them, and re-layouts  7.66 us
    pallas_call x8, Pallas kernels, finish(): pl.pallas_call(finish_kernel, grid=(1,), out_shape=jax.ShapeDtypeStruct(s...  5.39 us
    pallas_call x1, Pallas kernels, per_device(): pl.pallas_call(functools.partial(prep_kernel, chunk), out_shape=[struct((...  3.13 us
  transfers between devices with their start and end apart: 25, of which 7 were waited for; matrix products, arithmetic and copies ran while one was open for 0% of the time, Pallas kernels for 31%

profile of v1, /device:TPU:0, one launch (start us, length us, event | category | flops | bytes accessed | tf_op | source)
XLA Modules:
  0.0 91.4 jit_solution(4521353391912201257)
XLA Ops:
  0.0 1.2 %slice_select_fusion = (f32[7,64,256]{2,1,0:T(8,128)S(1)}, f32[7,64,256]{2,1,0:T(8,128)S(1)}) fusion(f32[16,64,256]{2,1,0:T(8,128)} %est.3, pred[]{:T(512)S(6)} %eq.5), kind=kLoop, calls=%fused_computation | loop fusion | flops 229376 | bytes 1835009 | tf_op jit(solution)/shard_map/jit(_where)/select_n | solution.py:263
  1.2 3.1 %collective-permute-start.1 = (f32[7,64,256]{2,1,0:T(8,128)S(1)}, f32[7,64,256]{2,1,0:T(8,128)S(1)}, u32[]{:S(2)}, u32[]{:S(2)}) collective-permute-start(f32[7,64,256]{2,1,0:T(8,128)S(1)} %get-tuple-element.53), channel_id=1, source_target_pairs={{0,1},{1,0},{2,3},{3,2},{4,8},{5,9},{6,10},{7,11},{8,4},{9,5},{10,... | collective-permute-start | bytes 1376264 | tf_op jit(solution)/shard_map/est_b/ppermute | solution.py:258
  4.4 0.1 collective-permute-start
  4.4 1.2 %copy-done.6 = f32[16,64,256]{2,1,0:T(8,128)S(1)} copy-done((f32[16,64,256]{2,1,0:T(8,128)S(1)}, f32[16,64,256]{2,1,0:T(8,128)}, u32[]{:S(2)}) %copy-start.6) | copy-done | bytes 1048600
  5.6 3.1 %prep.1 = (bf16[4,4,256,256]{3,2,1,0:T(8,128)(2,1)S(1)}, bf16[4,4,256,256]{3,2,1,0:T(8,128)(2,1)S(1)}, bf16[4,128,256]{2,1,0:T(8,128)(2,1)S(1)}, bf16[4,256,256]{2,1,0:T(8,128)(2,1)S(1)}, f32[2,16,64,256]{3,2,1,0:T(8,128)S(1)}) custom-call(f32[2,4,15]{2,1,0:T(4,128)} %refs_0_.1, f32[2,4,15]{2,1,0:T(4,128)} %refs_1_.1, f32[2,4,15]{2,1,0:T(4,128)} %refs_2_.1, ...), custom_call_target="tpu_custom_call" | custom-call | flops 2536715008 | bytes 4000000 | tf_op jit(solution)/shard_map/prep/pallas_call | solution.py:267
  8.8 2.0 %collective-permute-done.1.got_b = f32[7,64,256]{2,1,0:T(8,128)S(1)} collective-permute-done((f32[7,64,256]{2,1,0:T(8,128)S(1)}, f32[7,64,256]{2,1,0:T(8,128)S(1)}, u32[]{:S(2)}, u32[]{:S(2)}) %collective-permute-start.1) | collective-permute-done | bytes 458784 | tf_op jit(solution)/shard_map/est_b/ppermute | solution.py:258
  10.8 0.0 collective-permute-done.got_a
  10.8 6.7 %forward0.1 = (f32[16,64,256]{2,1,0:T(8,128)S(1)}, f32[7,64,256]{2,1,0:T(8,128)}, f32[7,64,256]{2,1,0:T(8,128)}) custom-call(f32[16,64,256]{2,1,0:T(8,128)S(1)} %copy-done.6, f32[7,64,256]{2,1,0:T(8,128)S(1)} %collective-permute-done.got_a, f32[7,64,256]{2,1,0:T(8,128)S(1)} %collective-permute-done.1.got_b, f32[2,16,64,256]{3,2,1,0:T(8,128)S(1)} %copy-done.7, ...), custom_call_target="tpu_custom_call" | custom-call | flops 3623878656 | bytes 4000000 | tf_op jit(solution)/shard_map/fwd0/forward0/pallas_call | solution.py:296
  17.5 1.0 %copy-done.8 = f32[16,64,256]{2,1,0:T(8,128)} copy-done((f32[16,64,256]{2,1,0:T(8,128)}, f32[16,64,256]{2,1,0:T(8,128)S(1)}, u32[]{:S(2)}) %copy-start.8) | copy-done | bytes 1048600
  18.5 0.1 collective-permute-start.4
  18.6 2.0 %collective-permute-start.5 = (f32[7,64,256]{2,1,0:T(8,128)}, f32[7,64,256]{2,1,0:T(8,128)}, u32[]{:S(2)}, u32[]{:S(2)}) collective-permute-start(f32[7,64,256]{2,1,0:T(8,128)} %get-tuple-element.34), channel_id=1, source_target_pairs={{0,1},{1,0},{2,3},{3,2},{4,8},{5,9},{6,10},{7,11},{8,4},{9,5},{10,... | collective-permute-start | bytes 1376264 | tf_op jit(solution)/shard_map/ratio0_b/ppermute | solution.py:258
  20.5 6.7 %forward1.1 = (f32[16,64,256]{2,1,0:T(8,128)S(1)}, f32[7,64,256]{2,1,0:T(8,128)}, f32[7,64,256]{2,1,0:T(8,128)}) custom-call(f32[16,64,256]{2,1,0:T(8,128)S(1)} %copy-done.6, f32[7,64,256]{2,1,0:T(8,128)S(1)} %collective-permute-done.got_a, f32[7,64,256]{2,1,0:T(8,128)S(1)} %collective-permute-done.1.got_b, f32[2,16,64,256]{3,2,1,0:T(8,128)S(1)} %copy-done.7, ...), custom_call_target="tpu_custom_call" | custom-call | flops 3623878656 | bytes 4000000 | tf_op jit(solution)/shard_map/fwd1/forward1/pallas_call | solution.py:296
  27.2 1.1 %collective-permute-start.3 = (f32[7,64,256]{2,1,0:T(8,128)}, f32[7,64,256]{2,1,0:T(8,128)}, u32[]{:S(2)}, u32[]{:S(2)}) collective-permute-start(f32[7,64,256]{2,1,0:T(8,128)} %get-tuple-element.30), channel_id=1, source_target_pairs={{0,1},{1,0},{2,3},{3,2},{4,8},{5,9},{6,10},{7,11},{8,4},{9,5},{10,... | collective-permute-start | bytes 1376264 | tf_op jit(solution)/shard_map/ratio1_b/ppermute | solution.py:258
  28.3 0.0 collective-permute-done.4.refs_1_
  28.3 0.0 collective-permute-done.5.refs_2_
  28.3 1.6 %copy-done.1 = bf16[4,4,256,256]{3,2,1,0:T(8,128)(2,1)S(1)} copy-done((bf16[4,4,256,256]{3,2,1,0:T(8,128)(2,1)S(1)}, bf16[4,4,256,256]{3,2,1,0:T(8,128)(2,1)}, u32[]{:S(2)}) %copy-start.1) | copy-done | bytes 2097176
  29.9 1.6 %copy-done.3 = f32[2,16,64,256]{3,2,1,0:T(8,128)S(1)} copy-done((f32[2,16,64,256]{3,2,1,0:T(8,128)S(1)}, f32[2,16,64,256]{3,2,1,0:T(8,128)}, u32[]{:S(2)}) %copy-start.3) | copy-done | bytes 2097176
  31.5 1.0 %copy-done.5 = bf16[4,256,256]{2,1,0:T(8,128)(2,1)S(1)} copy-done((bf16[4,256,256]{2,1,0:T(8,128)(2,1)S(1)}, bf16[4,256,256]{2,1,0:T(8,128)(2,1)}, u32[]{:S(2)}) %copy-start.5) | copy-done | bytes 524312
  32.5 1.2 %copy-done.9 = f32[16,64,256]{2,1,0:T(8,128)S(1)} copy-done((f32[16,64,256]{2,1,0:T(8,128)S(1)}, f32[16,64,256]{2,1,0:T(8,128)}, u32[]{:S(2)}) %copy-start.9) | copy-done | bytes 1048600
  33.7 5.9 %early.1.refs_8_ = f32[16,64,256]{2,1,0:T(8,128)S(1)} custom-call(f32[16,64,256]{2,1,0:T(8,128)S(1)} %copy-done.9, f32[7,64,256]{2,1,0:T(8,128)} %collective-permute-done.4.refs_1_, f32[7,64,256]{2,1,0:T(8,128)} %collective-permute-done.5.refs_2_, f32[2,16,64,256]{3,2,1,0:T(8,128)S(1)} %copy-done.3, ...), custom_call_target="tpu_custom_call" | custom-call | flops 3623878656 | bytes 4000000 | tf_op jit(solution)/shard_map/early/early/pallas_call | solution.py:335
  39.7 2.5 %back0.1 = (f32[2,64,256]{2,1,0:T(8,128)S(1)}, f32[2,64,256]{2,1,0:T(8,128)S(1)}) custom-call(f32[16,64,256]{2,1,0:T(8,128)S(1)} %get-tuple-element.28.refs_0_, f32[7,64,256]{2,1,0:T(8,128)} %collective-permute-done.2.refs_1_, f32[7,64,256]{2,1,0:T(8,128)} %collective-permute-done.3.refs_2_, f32[2,16,64,256]{3,2,1,0:T(8,128)S(1)} %copy-done.3, ...), custom_call_target="tpu_custom_call" | custom-call | flops 905969664 | bytes 4000000 | tf_op jit(solution)/shard_map/back0/back0/pallas_call | solution.py:335
  42.2 1.1 %collective-permute-start.13 = (f32[2,64,256]{2,1,0:T(8,128)S(1)}, f32[2,64,256]{2,1,0:T(8,128)S(1)}, u32[]{:S(2)}, u32[]{:S(2)}) collective-permute-start(f32[2,64,256]{2,1,0:T(8,128)S(1)} %get-tuple-element.41), channel_id=1, source_target_pairs={{0,1},{1,0},{2,3},{3,2},{4,5},{5,4},{6,7},{7,6},{8,9},{9,8},{10,11... | collective-permute-start | bytes 393224 | tf_op jit(solution)/shard_map/out0x/ppermute | solution.py:258
  43.3 1.0 %collective-permute-start.6 = (f32[2,64,256]{2,1,0:T(8,128)S(1)}, f32[2,64,256]{2,1,0:T(8,128)S(1)}, u32[]{:S(2)}, u32[]{:S(2)}) collective-permute-start(f32[2,64,256]{2,1,0:T(8,128)S(1)} %get-tuple-element.35.refs_9_), channel_id=1, source_target_pairs={{0,1},{1,0},{2,3},{3,2},{4,5},{5,4},{6,7},{7,6},{8,9},{9,8},{10,11... | collective-permute-start | bytes 393224 | tf_op jit(solution)/shard_map/out1x/ppermute | solution.py:258
  44.3 2.5 %back1.1 = (f32[2,64,256]{2,1,0:T(8,128)S(1)}, f32[2,64,256]{2,1,0:T(8,128)S(1)}) custom-call(f32[16,64,256]{2,1,0:T(8,128)S(1)} %get-tuple-element.28.refs_0_, f32[7,64,256]{2,1,0:T(8,128)} %collective-permute-done.2.refs_1_, f32[7,64,256]{2,1,0:T(8,128)} %collective-permute-done.3.refs_2_, f32[2,16,64,256]{3,2,1,0:T(8,128)S(1)} %copy-done.3, ...), custom_call_target="tpu_custom_call" | custom-call | flops 905969664 | bytes 4000000 | tf_op jit(solution)/shard_map/back1/back1/pallas_call | solution.py:335
  46.8 1.1 %collective-permute-start.20 = (f32[2,64,256]{2,1,0:T(8,128)S(1)}, f32[2,64,256]{2,1,0:T(8,128)S(1)}, u32[]{:S(2)}, u32[]{:S(2)}) collective-permute-start(f32[2,64,256]{2,1,0:T(8,128)S(1)} %get-tuple-element.42), channel_id=1, source_target_pairs={{0,1},{1,0},{2,3},{3,2},{4,5},{5,4},{6,7},{7,6},{8,9},{9,8},{10,11... | collective-permute-start | bytes 393224 | tf_op jit(solution)/shard_map/out2x/ppermute | solution.py:258
  47.9 2.5 %back2.1 = (f32[2,64,256]{2,1,0:T(8,128)S(1)}, f32[2,64,256]{2,1,0:T(8,128)S(1)}) custom-call(f32[16,64,256]{2,1,0:T(8,128)S(1)} %get-tuple-element.28.refs_0_, f32[7,64,256]{2,1,0:T(8,128)} %collective-permute-done.2.refs_1_, f32[7,64,256]{2,1,0:T(8,128)} %collective-permute-done.3.refs_2_, f32[2,16,64,256]{3,2,1,0:T(8,128)S(1)} %copy-done.3, ...), custom_call_target="tpu_custom_call" | custom-call | flops 905969664 | bytes 4000000 | tf_op jit(solution)/shard_map/back2/back2/pallas_call | solution.py:335
  50.3 2.5 %back3.1 = (f32[2,64,256]{2,1,0:T(8,128)S(1)}, f32[2,64,256]{2,1,0:T(8,128)S(1)}) custom-call(f32[16,64,256]{2,1,0:T(8,128)S(1)} %get-tuple-element.28.refs_0_, f32[7,64,256]{2,1,0:T(8,128)} %collective-permute-done.2.refs_1_, f32[7,64,256]{2,1,0:T(8,128)} %collective-permute-done.3.refs_2_, f32[2,16,64,256]{3,2,1,0:T(8,128)S(1)} %copy-done.3, ...), custom_call_target="tpu_custom_call" | custom-call | flops 905969664 | bytes 4000000 | tf_op jit(solution)/shard_map/back3/back3/pallas_call | solution.py:335
  52.8 0.0 collective-permute-done.13
  52.9 0.1 collective-permute-start.14
  52.9 0.6 collective-permute-done.20
  53.5 0.1 collective-permute-start.21
  53.6 0.0 collective-permute-done.6
  53.6 0.5 collective-permute-start.7
  54.2 0.1 collective-permute-done.14
  54.3 6.1 %collective-permute-start.15 = (f32[2,64,256]{2,1,0:T(8,128)S(1)}, f32[2,64,256]{2,1,0:T(8,128)S(1)}, u32[]{:S(2)}, u32[]{:S(2)}) collective-permute-start(f32[2,64,256]{2,1,0:T(8,128)S(1)} %get-tuple-element.47), channel_id=1, source_target_pairs={{0,1},{1,0},{2,3},{3,2},{4,5},{5,4},{6,7},{7,6},{8,9},{9,8},{10,11... | collective-permute-start | bytes 393224 | tf_op jit(solution)/shard_map/out3x/ppermute | solution.py:258
  60.5 2.8 %collective-permute-start.22 = (f32[2,64,256]{2,1,0:T(8,128)S(1)}, f32[2,64,256]{2,1,0:T(8,128)S(1)}, u32[]{:S(2)}, u32[]{:S(2)}) collective-permute-start(f32[2,64,256]{2,1,0:T(8,128)S(1)} %get-tuple-element.43), channel_id=1, source_target_pairs={{0,1},{1,0},{2,3},{3,2},{4,5},{5,4},{6,7},{7,6},{8,9},{9,8},{10,11... | collective-permute-start | bytes 393224 | tf_op jit(solution)/shard_map/out5x/ppermute | solution.py:258
  63.2 0.0 collective-permute-done.7
  63.3 1.5 %collective-permute-start.8 = (f32[2,64,256]{2,1,0:T(8,128)S(1)}, f32[2,64,256]{2,1,0:T(8,128)S(1)}, u32[]{:S(2)}, u32[]{:S(2)}) collective-permute-start(f32[2,64,256]{2,1,0:T(8,128)S(1)} %get-tuple-element.51), channel_id=1, source_target_pairs={{0,1},{1,0},{2,3},{3,2},{4,5},{5,4},{6,7},{7,6},{8,9},{9,8},{10,11... | collective-permute-start | bytes 393224 | tf_op jit(solution)/shard_map/out4x/ppermute | solution.py:258
  64.8 0.1 collective-permute-start.16
  64.9 2.4 %collective-permute-done.22.got = f32[2,64,256]{2,1,0:T(8,128)S(1)} collective-permute-done((f32[2,64,256]{2,1,0:T(8,128)S(1)}, f32[2,64,256]{2,1,0:T(8,128)S(1)}, u32[]{:S(2)}, u32[]{:S(2)}) %collective-permute-start.22) | collective-permute-done | bytes 131104 | tf_op jit(solution)/shard_map/out5x/ppermute | solution.py:258
  67.3 0.1 collective-permute-start.23
  67.4 1.3 %collective-permute-done.8.got = f32[2,64,256]{2,1,0:T(8,128)S(1)} collective-permute-done((f32[2,64,256]{2,1,0:T(8,128)S(1)}, f32[2,64,256]{2,1,0:T(8,128)S(1)}, u32[]{:S(2)}, u32[]{:S(2)}) %collective-permute-start.8) | collective-permute-done | bytes 131104 | tf_op jit(solution)/shard_map/out4x/ppermute | solution.py:258
  68.7 0.1 collective-permute-start.9
  68.8 0.0 collective-permute-done.16
  68.8 3.1 %collective-permute-start.17 = (f32[2,64,256]{2,1,0:T(8,128)S(1)}, f32[2,64,256]{2,1,0:T(8,128)S(1)}, u32[]{:S(2)}, u32[]{:S(2)}) collective-permute-start(f32[2,64,256]{2,1,0:T(8,128)S(1)} %get-tuple-element.45), channel_id=1, source_target_pairs={{0,1},{1,0},{2,3},{3,2},{4,5},{5,4},{6,7},{7,6},{8,9},{9,8},{10,11... | collective-permute-start | bytes 393224 | tf_op jit(solution)/shard_map/out6x/ppermute | solution.py:258
  72.0 2.2 %collective-permute-start.24 = (f32[2,64,256]{2,1,0:T(8,128)S(1)}, f32[2,64,256]{2,1,0:T(8,128)S(1)}, u32[]{:S(2)}, u32[]{:S(2)}) collective-permute-start(f32[2,64,256]{2,1,0:T(8,128)S(1)} %add_select_fusion.own), channel_id=1, source_target_pairs={{0,1},{1,0},{2,3},{3,2},{4,5},{5,4},{6,7},{7,6},{8,9},{9,8},{10,11... | collective-permute-start | bytes 393224 | tf_op jit(solution)/shard_map/out8x/ppermute | solution.py:258
  74.2 1.4 %collective-permute-start.10 = (f32[2,64,256]{2,1,0:T(8,128)S(1)}, f32[2,64,256]{2,1,0:T(8,128)S(1)}, u32[]{:S(2)}, u32[]{:S(2)}) collective-permute-start(f32[2,64,256]{2,1,0:T(8,128)S(1)} %get-tuple-element.49), channel_id=1, source_target_pairs={{0,1},{1,0},{2,3},{3,2},{4,5},{5,4},{6,7},{7,6},{8,9},{9,8},{10,11... | collective-permute-start | bytes 393224 | tf_op jit(solution)/shard_map/out7x/ppermute | solution.py:258
  75.6 0.7 collective-permute-done.17.got
  76.4 0.1 collective-permute-start.18
  76.4 4.0 %collective-permute-done.10.got = f32[2,64,256]{2,1,0:T(8,128)S(1)} collective-permute-done((f32[2,64,256]{2,1,0:T(8,128)S(1)}, f32[2,64,256]{2,1,0:T(8,128)S(1)}, u32[]{:S(2)}, u32[]{:S(2)}) %collective-permute-start.10) | collective-permute-done | bytes 131104 | tf_op jit(solution)/shard_map/out7x/ppermute | solution.py:258
  80.4 0.1 collective-permute-start.11
  80.6 3.6 %collective-permute-start.19 = (f32[2,64,256]{2,1,0:T(8,128)S(1)}, f32[2,64,256]{2,1,0:T(8,128)S(1)}, u32[]{:S(2)}, u32[]{:S(2)}) collective-permute-start(f32[2,64,256]{2,1,0:T(8,128)S(1)} %add_select_fusion.4.own), channel_id=1, source_target_pairs={{0,1},{1,0},{2,3},{3,2},{4,5},{5,4},{6,7},{7,6},{8,9},{9,8},{10,11... | collective-permute-start | bytes 393224 | tf_op jit(solution)/shard_map/out9x/ppermute | solution.py:258
  84.1 0.0 collective-permute-done.11
  84.2 1.8 %collective-permute-start.12 = (f32[2,64,256]{2,1,0:T(8,128)S(1)}, f32[2,64,256]{2,1,0:T(8,128)S(1)}, u32[]{:S(2)}, u32[]{:S(2)}) collective-permute-start(f32[2,64,256]{2,1,0:T(8,128)S(1)} %add_select_fusion.10.own), channel_id=1, source_target_pairs={{0,1},{1,0},{2,3},{3,2},{4,5},{5,4},{6,7},{7,6},{8,9},{9,8},{10,11... | collective-permute-start | bytes 393224 | tf_op jit(solution)/shard_map/out10x/ppermute | solution.py:258
  86.0 0.7 finish0.1.rest_0_
  86.7 0.7 finish1.1.rest_0_
  87.3 0.7 finish2.1.rest_0_
  88.0 0.7 finish3.1.rest_0_
  88.7 0.7 finish4.1.rest_0_
  89.4 0.7 finish5.1.rest_0_
  90.0 0.0 collective-permute-done.19.got
  90.1 0.7 finish6.1.rest_0_
  90.7 0.0 collective-permute-done.12.got
  90.7 0.7 finish7.1
  (39 shorter events, 0.4 us)
Async XLA Ops:
  1.2 9.6 %collective-permute-start.1 = (f32[7,64,256]{2,1,0:T(8,128)S(1)}, f32[7,64,256]{2,1,0:T(8,128)S(1)}, u32[]{:S(2)}, u32[]{:S(2)}) collective-permute-start(f32[7,64,256]{2,1,0:T(8,128)S(1)} %get-tuple-element.53), channel_id=1, source_target_pairs={{0,1},{1,0},{2,3},{3,2},{4,8},{5,9},{6,10},{7,11},{8,4},{9,5},{10,... | collective-permute-start | bytes 1376264 | tf_op jit(solution)/shard_map/est_b/ppermute | solution.py:258
  4.4 6.5 %collective-permute-start = (f32[7,64,256]{2,1,0:T(8,128)S(1)}, f32[7,64,256]{2,1,0:T(8,128)S(1)}, u32[]{:S(2)}, u32[]{:S(2)}) collective-permute-start(f32[7,64,256]{2,1,0:T(8,128)S(1)} %get-tuple-element.54), channel_id=1, source_target_pairs={{0,4},{1,5},{2,6},{3,7},{4,0},{5,1},{6,2},{7,3},{8,12},{9,13},{10,... | collective-permute-start | bytes 1376264 | tf_op jit(solution)/shard_map/est_a/ppermute | solution.py:258
  4.4 1.2 %copy-start.6 = (f32[16,64,256]{2,1,0:T(8,128)S(1)}, f32[16,64,256]{2,1,0:T(8,128)}, u32[]{:S(2)}) copy-start(f32[16,64,256]{2,1,0:T(8,128)} %est.3) | copy-start | bytes 3145732
  5.6 5.2 %copy-start.7 = (f32[2,16,64,256]{3,2,1,0:T(8,128)S(1)}, f32[2,16,64,256]{3,2,1,0:T(8,128)}, u32[]{:S(2)}) copy-start(f32[2,16,64,256]{3,2,1,0:T(8,128)} %measured.3) | copy-start | bytes 6291460
  8.8 8.8 %copy-start.2 = (f32[2,16,64,256]{3,2,1,0:T(8,128)}, f32[2,16,64,256]{3,2,1,0:T(8,128)S(1)}, u32[]{:S(2)}) copy-start(f32[2,16,64,256]{3,2,1,0:T(8,128)S(1)} %get-tuple-element.31.refs_3_) | copy-start | bytes 6291460
  8.8 11.7 %copy-start = (bf16[4,4,256,256]{3,2,1,0:T(8,128)(2,1)}, bf16[4,4,256,256]{3,2,1,0:T(8,128)(2,1)S(1)}, u32[]{:S(2)}) copy-start(bf16[4,4,256,256]{3,2,1,0:T(8,128)(2,1)S(1)} %get-tuple-element.25.rest_1_.refs_5_) | copy-start | bytes 6291460
  8.8 11.7 %copy-start.4 = (bf16[4,256,256]{2,1,0:T(8,128)(2,1)}, bf16[4,256,256]{2,1,0:T(8,128)(2,1)S(1)}, u32[]{:S(2)}) copy-start(bf16[4,256,256]{2,1,0:T(8,128)(2,1)S(1)} %get-tuple-element.27.rest_3_.refs_7_) | copy-start | bytes 1572868
  17.5 1.0 %copy-start.8 = (f32[16,64,256]{2,1,0:T(8,128)}, f32[16,64,256]{2,1,0:T(8,128)S(1)}, u32[]{:S(2)}) copy-start(f32[16,64,256]{2,1,0:T(8,128)S(1)} %get-tuple-element.32.refs_0_) | copy-start | bytes 3145732
  18.5 9.8 %collective-permute-start.4 = (f32[7,64,256]{2,1,0:T(8,128)}, f32[7,64,256]{2,1,0:T(8,128)}, u32[]{:S(2)}, u32[]{:S(2)}) collective-permute-start(f32[7,64,256]{2,1,0:T(8,128)} %get-tuple-element.33), channel_id=1, source_target_pairs={{0,4},{1,5},{2,6},{3,7},{4,0},{5,1},{6,2},{7,3},{8,12},{9,13},{10,... | collective-permute-start | bytes 1376264 | tf_op jit(solution)/shard_map/ratio0_a/ppermute | solution.py:258
  18.6 9.7 %collective-permute-start.5 = (f32[7,64,256]{2,1,0:T(8,128)}, f32[7,64,256]{2,1,0:T(8,128)}, u32[]{:S(2)}, u32[]{:S(2)}) collective-permute-start(f32[7,64,256]{2,1,0:T(8,128)} %get-tuple-element.34), channel_id=1, source_target_pairs={{0,1},{1,0},{2,3},{3,2},{4,8},{5,9},{6,10},{7,11},{8,4},{9,5},{10,... | collective-permute-start | bytes 1376264 | tf_op jit(solution)/shard_map/ratio0_b/ppermute | solution.py:258
  27.2 12.5 %collective-permute-start.2 = (f32[7,64,256]{2,1,0:T(8,128)}, f32[7,64,256]{2,1,0:T(8,128)}, u32[]{:S(2)}, u32[]{:S(2)}) collective-permute-start(f32[7,64,256]{2,1,0:T(8,128)} %get-tuple-element.29), channel_id=1, source_target_pairs={{0,4},{1,5},{2,6},{3,7},{4,0},{5,1},{6,2},{7,3},{8,12},{9,13},{10,... | collective-permute-start | bytes 1376264 | tf_op jit(solution)/shard_map/ratio1_a/ppermute | solution.py:258
  27.2 12.5 %collective-permute-start.3 = (f32[7,64,256]{2,1,0:T(8,128)}, f32[7,64,256]{2,1,0:T(8,128)}, u32[]{:S(2)}, u32[]{:S(2)}) collective-permute-start(f32[7,64,256]{2,1,0:T(8,128)} %get-tuple-element.30), channel_id=1, source_target_pairs={{0,1},{1,0},{2,3},{3,2},{4,8},{5,9},{6,10},{7,11},{8,4},{9,5},{10,... | collective-permute-start | bytes 1376264 | tf_op jit(solution)/shard_map/ratio1_b/ppermute | solution.py:258
  28.3 1.6 %copy-start.1 = (bf16[4,4,256,256]{3,2,1,0:T(8,128)(2,1)S(1)}, bf16[4,4,256,256]{3,2,1,0:T(8,128)(2,1)}, u32[]{:S(2)}) copy-start(bf16[4,4,256,256]{3,2,1,0:T(8,128)(2,1)} %copy-done) | copy-start | bytes 6291460
  29.9 1.6 %copy-start.3 = (f32[2,16,64,256]{3,2,1,0:T(8,128)S(1)}, f32[2,16,64,256]{3,2,1,0:T(8,128)}, u32[]{:S(2)}) copy-start(f32[2,16,64,256]{3,2,1,0:T(8,128)} %copy-done.2) | copy-start | bytes 6291460
  31.5 1.0 %copy-start.5 = (bf16[4,256,256]{2,1,0:T(8,128)(2,1)S(1)}, bf16[4,256,256]{2,1,0:T(8,128)(2,1)}, u32[]{:S(2)}) copy-start(bf16[4,256,256]{2,1,0:T(8,128)(2,1)} %copy-done.4) | copy-start | bytes 1572868
  32.5 1.2 %copy-start.9 = (f32[16,64,256]{2,1,0:T(8,128)S(1)}, f32[16,64,256]{2,1,0:T(8,128)}, u32[]{:S(2)}) copy-start(f32[16,64,256]{2,1,0:T(8,128)} %copy-done.8) | copy-start | bytes 3145732
  42.2 10.6 %collective-permute-start.13 = (f32[2,64,256]{2,1,0:T(8,128)S(1)}, f32[2,64,256]{2,1,0:T(8,128)S(1)}, u32[]{:S(2)}, u32[]{:S(2)}) collective-permute-start(f32[2,64,256]{2,1,0:T(8,128)S(1)} %get-tuple-element.41), channel_id=1, source_target_pairs={{0,1},{1,0},{2,3},{3,2},{4,5},{5,4},{6,7},{7,6},{8,9},{9,8},{10,11... | collective-permute-start | bytes 393224 | tf_op jit(solution)/shard_map/out0x/ppermute | solution.py:258
  43.3 10.3 %collective-permute-start.6 = (f32[2,64,256]{2,1,0:T(8,128)S(1)}, f32[2,64,256]{2,1,0:T(8,128)S(1)}, u32[]{:S(2)}, u32[]{:S(2)}) collective-permute-start(f32[2,64,256]{2,1,0:T(8,128)S(1)} %get-tuple-element.35.refs_9_), channel_id=1, source_target_pairs={{0,1},{1,0},{2,3},{3,2},{4,5},{5,4},{6,7},{7,6},{8,9},{9,8},{10,11... | collective-permute-start | bytes 393224 | tf_op jit(solution)/shard_map/out1x/ppermute | solution.py:258
  46.8 6.7 %collective-permute-start.20 = (f32[2,64,256]{2,1,0:T(8,128)S(1)}, f32[2,64,256]{2,1,0:T(8,128)S(1)}, u32[]{:S(2)}, u32[]{:S(2)}) collective-permute-start(f32[2,64,256]{2,1,0:T(8,128)S(1)} %get-tuple-element.42), channel_id=1, source_target_pairs={{0,1},{1,0},{2,3},{3,2},{4,5},{5,4},{6,7},{7,6},{8,9},{9,8},{10,11... | collective-permute-start | bytes 393224 | tf_op jit(solution)/shard_map/out2x/ppermute | solution.py:258
  52.9 1.4 %collective-permute-start.14 = (f32[2,64,256]{2,1,0:T(8,128)S(1)}, f32[2,64,256]{2,1,0:T(8,128)S(1)}, u32[]{:S(2)}, u32[]{:S(2)}) collective-permute-start(f32[2,64,256]{2,1,0:T(8,128)S(1)} %add_select_fusion.9), channel_id=1, source_target_pairs={{0,4},{1,2},{2,1},{3,7},{4,0},{5,6},{6,5},{7,3},{8,12},{9,10},{10,... | collective-permute-start | bytes 393224 | tf_op jit(solution)/shard_map/mid0x/ppermute | solution.py:258
  53.5 6.9 %collective-permute-start.21 = (f32[2,64,256]{2,1,0:T(8,128)S(1)}, f32[2,64,256]{2,1,0:T(8,128)S(1)}, u32[]{:S(2)}, u32[]{:S(2)}) collective-permute-start(f32[2,64,256]{2,1,0:T(8,128)S(1)} %add_select_fusion.3), channel_id=1, source_target_pairs={{0,4},{1,2},{2,1},{3,7},{4,0},{5,6},{6,5},{7,3},{8,12},{9,10},{10,... | collective-permute-start | bytes 393224 | tf_op jit(solution)/shard_map/mid2x/ppermute | solution.py:258
  53.6 9.6 %collective-permute-start.7 = (f32[2,64,256]{2,1,0:T(8,128)S(1)}, f32[2,64,256]{2,1,0:T(8,128)S(1)}, u32[]{:S(2)}, u32[]{:S(2)}) collective-permute-start(f32[2,64,256]{2,1,0:T(8,128)S(1)} %add_select_fusion.15), channel_id=1, source_target_pairs={{0,4},{1,2},{2,1},{3,7},{4,0},{5,6},{6,5},{7,3},{8,12},{9,10},{10,... | collective-permute-start | bytes 393224 | tf_op jit(solution)/shard_map/mid1x/ppermute | solution.py:258
  54.3 10.5 %collective-permute-start.15 = (f32[2,64,256]{2,1,0:T(8,128)S(1)}, f32[2,64,256]{2,1,0:T(8,128)S(1)}, u32[]{:S(2)}, u32[]{:S(2)}) collective-permute-start(f32[2,64,256]{2,1,0:T(8,128)S(1)} %get-tuple-element.47), channel_id=1, source_target_pairs={{0,1},{1,0},{2,3},{3,2},{4,5},{5,4},{6,7},{7,6},{8,9},{9,8},{10,11... | collective-permute-start | bytes 393224 | tf_op jit(solution)/shard_map/out3x/ppermute | solution.py:258
  60.5 6.8 %collective-permute-start.22 = (f32[2,64,256]{2,1,0:T(8,128)S(1)}, f32[2,64,256]{2,1,0:T(8,128)S(1)}, u32[]{:S(2)}, u32[]{:S(2)}) collective-permute-start(f32[2,64,256]{2,1,0:T(8,128)S(1)} %get-tuple-element.43), channel_id=1, source_target_pairs={{0,1},{1,0},{2,3},{3,2},{4,5},{5,4},{6,7},{7,6},{8,9},{9,8},{10,11... | collective-permute-start | bytes 393224 | tf_op jit(solution)/shard_map/out5x/ppermute | solution.py:258
  63.3 5.4 %collective-permute-start.8 = (f32[2,64,256]{2,1,0:T(8,128)S(1)}, f32[2,64,256]{2,1,0:T(8,128)S(1)}, u32[]{:S(2)}, u32[]{:S(2)}) collective-permute-start(f32[2,64,256]{2,1,0:T(8,128)S(1)} %get-tuple-element.51), channel_id=1, source_target_pairs={{0,1},{1,0},{2,3},{3,2},{4,5},{5,4},{6,7},{7,6},{8,9},{9,8},{10,11... | collective-permute-start | bytes 393224 | tf_op jit(solution)/shard_map/out4x/ppermute | solution.py:258
  64.8 4.0 %collective-permute-start.16 = (f32[2,64,256]{2,1,0:T(8,128)S(1)}, f32[2,64,256]{2,1,0:T(8,128)S(1)}, u32[]{:S(2)}, u32[]{:S(2)}) collective-permute-start(f32[2,64,256]{2,1,0:T(8,128)S(1)} %add_select_fusion.7), channel_id=1, source_target_pairs={{0,4},{1,2},{2,1},{3,7},{4,0},{5,6},{6,5},{7,3},{8,12},{9,10},{10,... | collective-permute-start | bytes 393224 | tf_op jit(solution)/shard_map/mid3x/ppermute | solution.py:258
  67.3 4.7 %collective-permute-start.23 = (f32[2,64,256]{2,1,0:T(8,128)S(1)}, f32[2,64,256]{2,1,0:T(8,128)S(1)}, u32[]{:S(2)}, u32[]{:S(2)}) collective-permute-start(f32[2,64,256]{2,1,0:T(8,128)S(1)} %add_select_fusion.1), channel_id=1, source_target_pairs={{0,4},{1,2},{2,1},{3,7},{4,0},{5,6},{6,5},{7,3},{8,12},{9,10},{10,... | collective-permute-start | bytes 393224 | tf_op jit(solution)/shard_map/mid5x/ppermute | solution.py:258
  68.7 5.5 %collective-permute-start.9 = (f32[2,64,256]{2,1,0:T(8,128)S(1)}, f32[2,64,256]{2,1,0:T(8,128)S(1)}, u32[]{:S(2)}, u32[]{:S(2)}) collective-permute-start(f32[2,64,256]{2,1,0:T(8,128)S(1)} %add_select_fusion.13), channel_id=1, source_target_pairs={{0,4},{1,2},{2,1},{3,7},{4,0},{5,6},{6,5},{7,3},{8,12},{9,10},{10,... | collective-permute-start | bytes 393224 | tf_op jit(solution)/shard_map/mid4x/ppermute | solution.py:258
  68.8 7.5 %collective-permute-start.17 = (f32[2,64,256]{2,1,0:T(8,128)S(1)}, f32[2,64,256]{2,1,0:T(8,128)S(1)}, u32[]{:S(2)}, u32[]{:S(2)}) collective-permute-start(f32[2,64,256]{2,1,0:T(8,128)S(1)} %get-tuple-element.45), channel_id=1, source_target_pairs={{0,1},{1,0},{2,3},{3,2},{4,5},{5,4},{6,7},{7,6},{8,9},{9,8},{10,11... | collective-permute-start | bytes 393224 | tf_op jit(solution)/shard_map/out6x/ppermute | solution.py:258
  72.0 17.4 %collective-permute-start.24 = (f32[2,64,256]{2,1,0:T(8,128)S(1)}, f32[2,64,256]{2,1,0:T(8,128)S(1)}, u32[]{:S(2)}, u32[]{:S(2)}) collective-permute-start(f32[2,64,256]{2,1,0:T(8,128)S(1)} %add_select_fusion.own), channel_id=1, source_target_pairs={{0,1},{1,0},{2,3},{3,2},{4,5},{5,4},{6,7},{7,6},{8,9},{9,8},{10,11... | collective-permute-start | bytes 393224 | tf_op jit(solution)/shard_map/out8x/ppermute | solution.py:258
  74.2 6.2 %collective-permute-start.10 = (f32[2,64,256]{2,1,0:T(8,128)S(1)}, f32[2,64,256]{2,1,0:T(8,128)S(1)}, u32[]{:S(2)}, u32[]{:S(2)}) collective-permute-start(f32[2,64,256]{2,1,0:T(8,128)S(1)} %get-tuple-element.49), channel_id=1, source_target_pairs={{0,1},{1,0},{2,3},{3,2},{4,5},{5,4},{6,7},{7,6},{8,9},{9,8},{10,11... | collective-permute-start | bytes 393224 | tf_op jit(solution)/shard_map/out7x/ppermute | solution.py:258
  76.4 4.2 %collective-permute-start.18 = (f32[2,64,256]{2,1,0:T(8,128)S(1)}, f32[2,64,256]{2,1,0:T(8,128)S(1)}, u32[]{:S(2)}, u32[]{:S(2)}) collective-permute-start(f32[2,64,256]{2,1,0:T(8,128)S(1)} %add_select_fusion.5), channel_id=1, source_target_pairs={{0,4},{1,2},{2,1},{3,7},{4,0},{5,6},{6,5},{7,3},{8,12},{9,10},{10,... | collective-permute-start | bytes 393224 | tf_op jit(solution)/shard_map/mid6x/ppermute | solution.py:258
  80.4 3.7 %collective-permute-start.11 = (f32[2,64,256]{2,1,0:T(8,128)S(1)}, f32[2,64,256]{2,1,0:T(8,128)S(1)}, u32[]{:S(2)}, u32[]{:S(2)}) collective-permute-start(f32[2,64,256]{2,1,0:T(8,128)S(1)} %add_select_fusion.11), channel_id=1, source_target_pairs={{0,4},{1,2},{2,1},{3,7},{4,0},{5,6},{6,5},{7,3},{8,12},{9,10},{10,... | collective-permute-start | bytes 393224 | tf_op jit(solution)/shard_map/mid7x/ppermute | solution.py:258
  80.6 9.5 %collective-permute-start.19 = (f32[2,64,256]{2,1,0:T(8,128)S(1)}, f32[2,64,256]{2,1,0:T(8,128)S(1)}, u32[]{:S(2)}, u32[]{:S(2)}) collective-permute-start(f32[2,64,256]{2,1,0:T(8,128)S(1)} %add_select_fusion.4.own), channel_id=1, source_target_pairs={{0,1},{1,0},{2,3},{3,2},{4,5},{5,4},{6,7},{7,6},{8,9},{9,8},{10,11... | collective-permute-start | bytes 393224 | tf_op jit(solution)/shard_map/out9x/ppermute | solution.py:258
  84.2 6.6 %collective-permute-start.12 = (f32[2,64,256]{2,1,0:T(8,128)S(1)}, f32[2,64,256]{2,1,0:T(8,128)S(1)}, u32[]{:S(2)}, u32[]{:S(2)}) collective-permute-start(f32[2,64,256]{2,1,0:T(8,128)S(1)} %add_select_fusion.10.own), channel_id=1, source_target_pairs={{0,1},{1,0},{2,3},{3,2},{4,5},{5,4},{6,7},{7,6},{8,9},{9,8},{10,11... | collective-permute-start | bytes 393224 | tf_op jit(solution)/shard_map/out10x/ppermute | solution.py:258

commit v2 on v1

--- a/solution.py
+++ b/solution.py
@@ -11,7 +11,7 @@
 f32 = jnp.float32
 bf16 = jnp.bfloat16
 SUB = 8
-VMEM_LIMIT = 13 * 2**20
+VMEM_LIMIT = 24 * 2**20
 
 
 def split(values):
@@ -114,26 +114,16 @@
             scale[m, z] = est[z] * (weight / (grand * normal))
 
 
-def load_split(own, got, first, last, high, low):
-    radius, planes = got[0].shape[0], own.shape[0]
-    slab, slabs = lax.axis_index("slab"), lax.axis_size("slab")
-    even = lax.rem(slab, 2) == 0
-
-    def before(a, b, rows):
-        piece = jnp.where(even, got[1][a:b, rows, :], got[0][a:b, rows, :])
-        return jnp.where(slab > 0, piece, 0.0)
-
-    def after(a, b, rows):
-        piece = jnp.where(even, got[0][a:b, rows, :], got[1][a:b, rows, :])
-        return jnp.where(slab < slabs - 1, piece, 0.0)
-
-    sources = [(0, radius, before), (radius, planes, lambda a, b, rows: own[a:b, rows, :]), (radius + planes, radius, after)]
+def load_split(pieces, first, last, high, low):
+    starts = [0]
+    for piece in pieces:
+        starts.append(starts[-1] + piece.shape[0])
     for block in range(high.shape[0]):
         parts = []
-        for start, count, read in sources:
-            a, b = max(first - start, 0), min(last - start, count)
+        for piece, start in zip(pieces, starts):
+            a, b = max(first - start, 0), min(last - start, piece.shape[0])
             if a < b:
-                parts.append(read(a, b, slice(block * SUB, (block + 1) * SUB)))
+                parts.append(piece[a:b, block * SUB : (block + 1) * SUB, :])
         rows = jnp.concatenate(parts, axis=0)
         rows = rows.reshape((last - first) * SUB, rows.shape[2])
         h, l = split(rows)
@@ -172,14 +162,14 @@
     return results
 
 
-def forward_kernel(chunk, reach, est, got_a, got_b, measured, *rest):
-    mats, (ratio, send_a, send_b, high, low, *scratch) = rest[:4], rest[4:]
+def forward_kernel(chunk, reach, before, est, after, measured, *rest):
+    mats, (ratio, head, tail, high, low, *scratch) = rest[:4], rest[4:]
     c = pl.program_id(0)
-    planes, radius = ratio.shape[0], send_a.shape[0]
+    planes = ratio.shape[0]
 
     @pl.when(c == 0)
     def _():
-        load_split(est, (got_a, got_b), 0, planes + reach, high, low)
+        load_split((before, est, after), 0, planes + reach, high, low)
 
     blurred = apply_chunk(c, chunk, reach, high, low, mats, scratch)
     for z in range(chunk):
@@ -187,10 +177,8 @@
 
     @pl.when(c == pl.num_programs(0) - 1)
     def _():
-        even = lax.rem(lax.axis_index("slab"), 2) == 0
-        head, tail = ratio[0:radius], ratio[planes - radius : planes]
-        send_a[...] = jnp.where(even, tail, head)
-        send_b[...] = jnp.where(even, head, tail)
+        head[...] = ratio[0 : head.shape[0]]
+        tail[...] = ratio[planes - tail.shape[0] : planes]
 
 
 def backward_kernel(chunk, reach, first, count, views, has_sum, has_after, *refs):
@@ -204,7 +192,7 @@
     high, low, *scratch = refs
     step = outs[0].shape[0]
     for i, (pieces, scale, mats) in enumerate(per_view):
-        load_split(pieces[0], pieces[1:], first * chunk, (first + count) * chunk + reach, high, low)
+        load_split(pieces, first * chunk, (first + count) * chunk + reach, high, low)
         for c in range(count):
             back = apply_chunk(c, chunk, reach, high, low, mats, scratch)
             for z in range(chunk):
@@ -218,12 +206,6 @@
                 out[place % step] = term
 
 
-def finish_kernel(got, own, *rest):
-    place, count = lax.axis_index("view"), lax.axis_size("view")
-    end = (place == 0) | (place == count - 1)
-    rest[-1][...] = jnp.where(end, got[...], own[...])
-
-
 def whole(shape):
     return pl.BlockSpec(shape, lambda *_: (0,) * len(shape))
 
@@ -249,7 +231,8 @@
         return pl.CostEstimate(flops=int(flops), bytes_accessed=int(4e6), transcendentals=0)
 
     slabs, line = lax.axis_size("slab"), lax.axis_size("view")
-    even = lax.rem(lax.axis_index("slab"), 2) == 0
+    slab = lax.axis_index("slab")
+    even = lax.rem(slab, 2) == 0
     across = [swaps(slabs, line, 0, 0), swaps(slabs, line, 0, 1)]
     along = [swaps(slabs, line, 1, 0), swaps(slabs, line, 1, 1)]
 
@@ -257,11 +240,14 @@
         with jax.named_scope(name):
             return lax.ppermute(send, ("slab", "view"), perm)
 
-    head, tail = estimate[:radius], estimate[planes - radius :]
-    got = [
-        exchange(jnp.where(even, tail, head), across[0], "est_a"),
-        exchange(jnp.where(even, head, tail), across[1], "est_b"),
-    ]
+    def neighbours(head, tail, name):
+        got_a = exchange(jnp.where(even, tail, head), across[0], name + "_a")
+        got_b = exchange(jnp.where(even, head, tail), across[1], name + "_b")
+        before = jnp.where(slab > 0, jnp.where(even, got_b, got_a), 0.0)
+        after = jnp.where(slab < slabs - 1, jnp.where(even, got_a, got_b), 0.0)
+        return before, after
+
+    before, after = neighbours(estimate[:radius], estimate[planes - radius :], "est")
     depth_lanes = -(-(chunk + reach) * SUB // 128) * 128
     slots = 2 * members
     mats_and_scale = pl.pallas_call(
@@ -293,14 +279,14 @@
     extended = []
     for m in range(members):
         with jax.named_scope(f"fwd{m}"):
-            ratio, send_a, send_b = pl.pallas_call(
+            ratio, head, tail = pl.pallas_call(
                 functools.partial(forward_kernel, chunk, reach),
                 grid=(chunks,),
                 out_shape=[struct((planes,) + plane, f32), struct((radius,) + plane, f32), struct((radius,) + plane, f32)],
                 in_specs=[
+                    whole(before.shape),
                     whole(estimate.shape),
-                    whole(got[0].shape),
-                    whole(got[1].shape),
+                    whole(after.shape),
                     pl.BlockSpec((None, chunk) + plane, lambda c, m=m: (m, c, 0, 0)),
                 ]
                 + [slot_of(a, 2 * m) for a in mats],
@@ -309,10 +295,9 @@
                 compiler_params=params,
                 cost_estimate=cost(1),
                 name=f"forward{m}",
-            )(estimate, *got, measured, *mats)
-        extended.append(
-            (ratio, exchange(send_a, across[0], f"ratio{m}_a"), exchange(send_b, across[1], f"ratio{m}_b"))
-        )
+            )(before, estimate, after, measured, *mats)
+        left, right = neighbours(head, tail, f"ratio{m}")
+        extended.append((left, ratio, right))
 
     def backward(views, first, count, running, after, piece, name):
         operands, specs = [], []
@@ -375,7 +360,7 @@
     depth = jnp.minimum(place, count - 1 - place)
     pieces = list(pieces)
     total = len(pieces)
-    out = None
+    out = jnp.zeros(shape, f32)
     for j in range(total + (last // 2) * LAG):
         for odd in range(2):
             live = [(j - (i // 2) * LAG, i) for i in range(odd, last + 1, 2)]
@@ -393,25 +378,11 @@
                     pieces[k] = jnp.where(depth == target, pieces[k] + got, pieces[k])
                 elif i < last:
                     pieces[k] = jnp.where(depth == last - i, got, pieces[k])
+                elif half > 1:
+                    pieces[k] = jnp.where(depth == 0, got, pieces[k])
                 if i == last:
-                    out = finish(got if half > 1 else pieces[k], pieces[k], out, k, shape)
+                    out = lax.dynamic_update_slice(out, pieces[k], (sum(sizes[:k]), 0, 0))
     return out
-
-
-def finish(got, own, out, k, shape):
-    block = pl.BlockSpec(own.shape, lambda *_: (k, 0, 0))
-    with jax.named_scope(f"finish{k}x"):
-        return pl.pallas_call(
-            finish_kernel,
-            grid=(1,),
-            out_shape=jax.ShapeDtypeStruct(shape, f32),
-            in_specs=[whole(got.shape), whole(own.shape)] + ([pl.BlockSpec(memory_space=pltpu.HBM)] if out is not None else []),
-            out_specs=block,
-            input_output_aliases={2: 0} if out is not None else {},
-            compiler_params=pltpu.CompilerParams(vmem_limit_bytes=2**22),
-            cost_estimate=pl.CostEstimate(flops=1000, bytes_accessed=12 * own.size, transcendentals=0),
-            name=f"finish{k}",
-        )(got, own, *([] if out is None else [out]))
 
 
 def swaps(slabs, line, axis, odd):

time: 91.9 us -> 83.4 us (0.908)
  Pallas kernels: 37.8 us -> 24.6 us
  waiting for transfers between devices: 11.1 us -> 18.8 us
  local copies, waits for them, and re-layouts: 7.66 us -> 1.33 us
  starting transfers between devices: 33 us -> 35.4 us
  other arithmetic: 1.59 us -> 2.77 us
    ppermute x25, waiting for transfers between devices: 11.1 us -> 18.8 us  [exchange(): return lax.ppermute(send, ('slab', 'view'), perm)]
    unnamed x20 -> x6, local copies, waits for them, and re-layouts: 7.66 us -> 1.23 us
    pallas_call x5, Pallas kernels: 15.8 us -> 10 us  [backward(): pl.pallas_call(functools.partial(backward_kernel, chunk, reach, first, co...]
    pallas_call x8 -> x0, Pallas kernels: 5.39 us -> none  [finish(): pl.pallas_call(finish_kernel, grid=(1,), out_shape=jax.ShapeDtypeStruct(s...]
    ppermute x25, starting transfers between devices: 33 us -> 35.4 us  [exchange(): return lax.ppermute(send, ('slab', 'view'), perm)]
    pallas_call x2, Pallas kernels: 13.4 us -> 11.4 us  [per_device(): pl.pallas_call(functools.partial(forward_kernel, chunk, reach), grid=(chu...]
  transfers between devices with their start and end apart: 25 -> 25, of which waited for: 7 -> 8; matrix products, arithmetic and copies ran while one was open for 0% -> 1% of each run, Pallas kernels for 31% -> 21%
where the time goes in v2:
time: 83.4 us; the launch traced here: 83.2 us
  starting transfers between devices  35.4 us (42%)
  Pallas kernels  24.6 us (29%)
  waiting for transfers between devices  18.8 us (23%)
  other arithmetic  2.77 us (3%)
  local copies, waits for them, and re-layouts  1.33 us (2%)
    ppermute x25, starting transfers between devices, exchange(): return lax.ppermute(send, ('slab', 'view'), perm)  35.4 us
    ppermute x25, waiting for transfers between devices, exchange(): return lax.ppermute(send, ('slab', 'view'), perm)  18.8 us
    pallas_call x2, Pallas kernels, per_device(): pl.pallas_call(functools.partial(forward_kernel, chunk, reach), grid=(chu...  11.4 us
    pallas_call x5, Pallas kernels, backward(): pl.pallas_call(functools.partial(backward_kernel, chunk, reach, first, co...  10 us
    pallas_call x1, Pallas kernels, per_device(): pl.pallas_call(functools.partial(prep_kernel, chunk), out_shape=[struct((...  3.13 us
  transfers between devices with their start and end apart: 25, of which 8 were waited for; matrix products, arithmetic and copies ran while one was open for 1% of the time, Pallas kernels for 21%

profile of v2, /device:TPU:0, one launch (start us, length us, event | category | flops | bytes accessed | tf_op | source)
XLA Modules:
  0.0 83.2 jit_solution(209592820297151824)
XLA Ops:
  0.0 1.2 %slice_select_fusion = (f32[7,64,256]{2,1,0:T(8,128)S(1)}, f32[7,64,256]{2,1,0:T(8,128)S(1)}) fusion(f32[16,64,256]{2,1,0:T(8,128)} %est.3, pred[]{:T(512)S(6)} %eq.8), kind=kLoop, calls=%fused_computation.6 | loop fusion | flops 229376 | bytes 1835009 | tf_op jit(solution)/shard_map/jit(_where)/select_n | solution.py:244
  1.3 0.6 collective-permute-start.1
  1.8 2.6 %collective-permute-start = (f32[7,64,256]{2,1,0:T(8,128)S(1)}, f32[7,64,256]{2,1,0:T(8,128)S(1)}, u32[]{:S(2)}, u32[]{:S(2)}) collective-permute-start(f32[7,64,256]{2,1,0:T(8,128)S(1)} %get-tuple-element.44), channel_id=1, source_target_pairs={{0,1},{1,0},{2,3},{3,2},{4,8},{5,9},{6,10},{7,11},{8,4},{9,5},{10,... | collective-permute-start | bytes 1376264 | tf_op jit(solution)/shard_map/est_b/ppermute | solution.py:241
  4.5 1.2 %copy-done = f32[16,64,256]{2,1,0:T(8,128)S(1)} copy-done((f32[16,64,256]{2,1,0:T(8,128)S(1)}, f32[16,64,256]{2,1,0:T(8,128)}, u32[]{:S(2)}) %copy-start) | copy-done | bytes 1048600
  5.7 3.1 %prep.1 = (bf16[4,4,256,256]{3,2,1,0:T(8,128)(2,1)S(1)}, bf16[4,4,256,256]{3,2,1,0:T(8,128)(2,1)S(1)}, bf16[4,128,256]{2,1,0:T(8,128)(2,1)S(1)}, bf16[4,256,256]{2,1,0:T(8,128)(2,1)S(1)}, f32[2,16,64,256]{3,2,1,0:T(8,128)S(1)}) custom-call(f32[2,4,15]{2,1,0:T(4,128)} %refs_0_.1, f32[2,4,15]{2,1,0:T(4,128)} %refs_1_.1, f32[2,4,15]{2,1,0:T(4,128)} %refs_2_.1, ...), custom_call_target="tpu_custom_call" | custom-call | flops 2536715008 | bytes 4000000 | tf_op jit(solution)/shard_map/prep/pallas_call | solution.py:253
  8.8 0.0 collective-permute-done.1
  8.8 2.1 %collective-permute-done = f32[7,64,256]{2,1,0:T(8,128)S(1)} collective-permute-done((f32[7,64,256]{2,1,0:T(8,128)S(1)}, f32[7,64,256]{2,1,0:T(8,128)S(1)}, u32[]{:S(2)}, u32[]{:S(2)}) %collective-permute-start) | collective-permute-done | bytes 458784 | tf_op jit(solution)/shard_map/est_b/ppermute | solution.py:241
  10.9 0.1 select_select_fusion.4
  11.0 5.6 %forward0.1 = (f32[16,64,256]{2,1,0:T(8,128)S(1)}, f32[7,64,256]{2,1,0:T(8,128)S(1)}, f32[7,64,256]{2,1,0:T(8,128)S(1)}) custom-call(f32[7,64,256]{2,1,0:T(8,128)S(1)} %get-tuple-element.54.before, f32[16,64,256]{2,1,0:T(8,128)S(1)} %copy-done, f32[7,64,256]{2,1,0:T(8,128)S(1)} %get-tuple-element.53.after, f32[2,16,64,256]{3,2,1,0:T(8,128)S(1)} %copy-done.1, ...), custom_call_target="tpu_custom_call" | custom-call | flops 3623878656 | bytes 4000000 | tf_op jit(solution)/shard_map/fwd0/forward0/pallas_call | solution.py:282
  16.7 0.1 broadcast_select_fusion
  16.8 0.1 collective-permute-start.5
  16.9 2.1 %collective-permute-start.4 = (f32[7,64,256]{2,1,0:T(8,128)S(1)}, f32[7,64,256]{2,1,0:T(8,128)S(1)}, u32[]{:S(2)}, u32[]{:S(2)}) collective-permute-start(f32[7,64,256]{2,1,0:T(8,128)S(1)} %get-tuple-element.48), channel_id=1, source_target_pairs={{0,1},{1,0},{2,3},{3,2},{4,8},{5,9},{6,10},{7,11},{8,4},{9,5},{10,... | collective-permute-start | bytes 1376264 | tf_op jit(solution)/shard_map/ratio0_b/ppermute | solution.py:241
  19.0 5.8 %forward1.1 = (f32[16,64,256]{2,1,0:T(8,128)S(1)}, f32[7,64,256]{2,1,0:T(8,128)S(1)}, f32[7,64,256]{2,1,0:T(8,128)S(1)}) custom-call(f32[7,64,256]{2,1,0:T(8,128)S(1)} %get-tuple-element.54.before, f32[16,64,256]{2,1,0:T(8,128)S(1)} %copy-done, f32[7,64,256]{2,1,0:T(8,128)S(1)} %get-tuple-element.53.after, f32[2,16,64,256]{3,2,1,0:T(8,128)S(1)} %copy-done.1, ...), custom_call_target="tpu_custom_call" | custom-call | flops 3623878656 | bytes 4000000 | tf_op jit(solution)/shard_map/fwd1/forward1/pallas_call | solution.py:282
  24.8 0.1 broadcast_select_fusion.2
  24.9 0.1 collective-permute-start.3
  24.9 1.0 %collective-permute-start.2 = (f32[7,64,256]{2,1,0:T(8,128)S(1)}, f32[7,64,256]{2,1,0:T(8,128)S(1)}, u32[]{:S(2)}, u32[]{:S(2)}) collective-permute-start(f32[7,64,256]{2,1,0:T(8,128)S(1)} %get-tuple-element.52), channel_id=1, source_target_pairs={{0,1},{1,0},{2,3},{3,2},{4,8},{5,9},{6,10},{7,11},{8,4},{9,5},{10,... | collective-permute-start | bytes 1376264 | tf_op jit(solution)/shard_map/ratio1_b/ppermute | solution.py:241
  26.0 0.0 collective-permute-done.5
  26.0 0.0 collective-permute-done.4
  26.0 0.1 select_select_fusion
  26.1 4.8 %early.1.refs_8_ = f32[16,64,256]{2,1,0:T(8,128)S(1)} custom-call(f32[7,64,256]{2,1,0:T(8,128)S(1)} %get-tuple-element.46.refs_0_, f32[16,64,256]{2,1,0:T(8,128)S(1)} %get-tuple-element.34.refs_1_, f32[7,64,256]{2,1,0:T(8,128)S(1)} %get-tuple-element.45.refs_2_, f32[2,16,64,256]{3,2,1,0:T(8,128)S(1)} %get-tuple-element.31.refs_3_, ...), custom_call_target="tpu_custom_call" | custom-call | flops 3623878656 | bytes 4000000 | tf_op jit(solution)/shard_map/early/early/pallas_call | solution.py:320
  30.8 0.0 collective-permute-done.3
  30.8 2.6 %collective-permute-done.2 = f32[7,64,256]{2,1,0:T(8,128)S(1)} collective-permute-done((f32[7,64,256]{2,1,0:T(8,128)S(1)}, f32[7,64,256]{2,1,0:T(8,128)S(1)}, u32[]{:S(2)}, u32[]{:S(2)}) %collective-permute-start.2) | collective-permute-done | bytes 458784 | tf_op jit(solution)/shard_map/ratio1_b/ppermute | solution.py:241
  33.5 0.1 select_select_fusion.2
  33.6 1.3 %back0.1 = (f32[2,64,256]{2,1,0:T(8,128)S(1)}, f32[2,64,256]{2,1,0:T(8,128)S(1)}) custom-call(f32[7,64,256]{2,1,0:T(8,128)S(1)} %get-tuple-element.50.refs_0_, f32[16,64,256]{2,1,0:T(8,128)S(1)} %get-tuple-element.30.refs_1_, f32[7,64,256]{2,1,0:T(8,128)S(1)} %get-tuple-element.49.refs_2_, f32[2,16,64,256]{3,2,1,0:T(8,128)S(1)} %get-tuple-element.31.refs_3_, ...), custom_call_target="tpu_custom_call" | custom-call | flops 905969664 | bytes 4000000 | tf_op jit(solution)/shard_map/back0/back0/pallas_call | solution.py:320
  34.9 1.0 %collective-permute-start.9 = (f32[2,64,256]{2,1,0:T(8,128)S(1)}, f32[2,64,256]{2,1,0:T(8,128)S(1)}, u32[]{:S(2)}, u32[]{:S(2)}) collective-permute-start(f32[2,64,256]{2,1,0:T(8,128)S(1)} %get-tuple-element.36.refs_9_), channel_id=1, source_target_pairs={{0,1},{1,0},{2,3},{3,2},{4,5},{5,4},{6,7},{7,6},{8,9},{9,8},{10,11... | collective-permute-start | bytes 393224 | tf_op jit(solution)/shard_map/out1x/ppermute | solution.py:241
  35.9 1.3 %back1.1 = (f32[2,64,256]{2,1,0:T(8,128)S(1)}, f32[2,64,256]{2,1,0:T(8,128)S(1)}) custom-call(f32[7,64,256]{2,1,0:T(8,128)S(1)} %get-tuple-element.50.refs_0_, f32[16,64,256]{2,1,0:T(8,128)S(1)} %get-tuple-element.30.refs_1_, f32[7,64,256]{2,1,0:T(8,128)S(1)} %get-tuple-element.49.refs_2_, f32[2,16,64,256]{3,2,1,0:T(8,128)S(1)} %get-tuple-element.31.refs_3_, ...), custom_call_target="tpu_custom_call" | custom-call | flops 905969664 | bytes 4000000 | tf_op jit(solution)/shard_map/back1/back1/pallas_call | solution.py:320
  37.3 1.1 %collective-permute-start.6 = (f32[2,64,256]{2,1,0:T(8,128)S(1)}, f32[2,64,256]{2,1,0:T(8,128)S(1)}, u32[]{:S(2)}, u32[]{:S(2)}) collective-permute-start(f32[2,64,256]{2,1,0:T(8,128)S(1)} %get-tuple-element.35), channel_id=1, source_target_pairs={{0,1},{1,0},{2,3},{3,2},{4,5},{5,4},{6,7},{7,6},{8,9},{9,8},{10,11... | collective-permute-start | bytes 393224 | tf_op jit(solution)/shard_map/out0x/ppermute | solution.py:241
  38.4 1.0 %collective-permute-start.12 = (f32[2,64,256]{2,1,0:T(8,128)S(1)}, f32[2,64,256]{2,1,0:T(8,128)S(1)}, u32[]{:S(2)}, u32[]{:S(2)}) collective-permute-start(f32[2,64,256]{2,1,0:T(8,128)S(1)} %get-tuple-element.39), channel_id=1, source_target_pairs={{0,1},{1,0},{2,3},{3,2},{4,5},{5,4},{6,7},{7,6},{8,9},{9,8},{10,11... | collective-permute-start | bytes 393224 | tf_op jit(solution)/shard_map/out2x/ppermute | solution.py:241
  39.4 1.3 %back2.1 = (f32[2,64,256]{2,1,0:T(8,128)S(1)}, f32[2,64,256]{2,1,0:T(8,128)S(1)}) custom-call(f32[7,64,256]{2,1,0:T(8,128)S(1)} %get-tuple-element.50.refs_0_, f32[16,64,256]{2,1,0:T(8,128)S(1)} %get-tuple-element.30.refs_1_, f32[7,64,256]{2,1,0:T(8,128)S(1)} %get-tuple-element.49.refs_2_, f32[2,16,64,256]{3,2,1,0:T(8,128)S(1)} %get-tuple-element.31.refs_3_, ...), custom_call_target="tpu_custom_call" | custom-call | flops 905969664 | bytes 4000000 | tf_op jit(solution)/shard_map/back2/back2/pallas_call | solution.py:320
  40.7 1.3 %back3.1 = (f32[2,64,256]{2,1,0:T(8,128)S(1)}, f32[2,64,256]{2,1,0:T(8,128)S(1)}) custom-call(f32[7,64,256]{2,1,0:T(8,128)S(1)} %get-tuple-element.50.refs_0_, f32[16,64,256]{2,1,0:T(8,128)S(1)} %get-tuple-element.30.refs_1_, f32[7,64,256]{2,1,0:T(8,128)S(1)} %get-tuple-element.49.refs_2_, f32[2,16,64,256]{3,2,1,0:T(8,128)S(1)} %get-tuple-element.31.refs_3_, ...), custom_call_target="tpu_custom_call" | custom-call | flops 905969664 | bytes 4000000 | tf_op jit(solution)/shard_map/back3/back3/pallas_call | solution.py:320
  42.0 2.1 %collective-permute-done.6 = f32[2,64,256]{2,1,0:T(8,128)S(1)} collective-permute-done((f32[2,64,256]{2,1,0:T(8,128)S(1)}, f32[2,64,256]{2,1,0:T(8,128)S(1)}, u32[]{:S(2)}, u32[]{:S(2)}) %collective-permute-start.6) | collective-permute-done | bytes 131104 | tf_op jit(solution)/shard_map/out0x/ppermute | solution.py:241
  44.1 0.1 collective-permute-start.7
  44.2 1.9 %collective-permute-done.12 = f32[2,64,256]{2,1,0:T(8,128)S(1)} collective-permute-done((f32[2,64,256]{2,1,0:T(8,128)S(1)}, f32[2,64,256]{2,1,0:T(8,128)S(1)}, u32[]{:S(2)}, u32[]{:S(2)}) %collective-permute-start.12) | collective-permute-done | bytes 131104 | tf_op jit(solution)/shard_map/out2x/ppermute | solution.py:241
  46.1 0.1 collective-permute-start.13
  46.2 0.0 collective-permute-done.9
  46.2 0.5 collective-permute-start.10
  46.8 0.0 collective-permute-done.7
  46.8 4.5 %collective-permute-start.8 = (f32[2,64,256]{2,1,0:T(8,128)S(1)}, f32[2,64,256]{2,1,0:T(8,128)S(1)}, u32[]{:S(2)}, u32[]{:S(2)}) collective-permute-start(f32[2,64,256]{2,1,0:T(8,128)S(1)} %broadcast_select_fusion.8), channel_id=1, source_target_pairs={{0,1},{1,0},{2,3},{3,2},{4,5},{5,4},{6,7},{7,6},{8,9},{9,8},{10,11... | collective-permute-start | bytes 393224 | tf_op jit(solution)/shard_map/out3x/ppermute | solution.py:241
  51.3 2.8 %collective-permute-start.14 = (f32[2,64,256]{2,1,0:T(8,128)S(1)}, f32[2,64,256]{2,1,0:T(8,128)S(1)}, u32[]{:S(2)}, u32[]{:S(2)}) collective-permute-start(f32[2,64,256]{2,1,0:T(8,128)S(1)} %broadcast_select_fusion.6), channel_id=1, source_target_pairs={{0,1},{1,0},{2,3},{3,2},{4,5},{5,4},{6,7},{7,6},{8,9},{9,8},{10,11... | collective-permute-start | bytes 393224 | tf_op jit(solution)/shard_map/out5x/ppermute | solution.py:241
  54.1 0.0 collective-permute-done.10
  54.1 1.9 %collective-permute-start.11 = (f32[2,64,256]{2,1,0:T(8,128)S(1)}, f32[2,64,256]{2,1,0:T(8,128)S(1)}, u32[]{:S(2)}, u32[]{:S(2)}) collective-permute-start(f32[2,64,256]{2,1,0:T(8,128)S(1)} %broadcast_select_fusion.7), channel_id=1, source_target_pairs={{0,1},{1,0},{2,3},{3,2},{4,5},{5,4},{6,7},{7,6},{8,9},{9,8},{10,11... | collective-permute-start | bytes 393224 | tf_op jit(solution)/shard_map/out4x/ppermute | solution.py:241
  56.0 0.0 collective-permute-done.8
  56.1 0.1 collective-permute-start.15
  56.1 0.1 dynamic_update_slice.24
  56.2 3.6 %collective-permute-done.11 = f32[2,64,256]{2,1,0:T(8,128)S(1)} collective-permute-done((f32[2,64,256]{2,1,0:T(8,128)S(1)}, f32[2,64,256]{2,1,0:T(8,128)S(1)}, u32[]{:S(2)}, u32[]{:S(2)}) %collective-permute-start.11) | collective-permute-done | bytes 131104 | tf_op jit(solution)/shard_map/out4x/ppermute | solution.py:241
  59.9 0.0 collective-permute-done.14
  59.9 0.1 collective-permute-start.19
  60.0 0.5 collective-permute-start.17
  60.5 3.6 %collective-permute-start.16 = (f32[2,64,256]{2,1,0:T(8,128)S(1)}, f32[2,64,256]{2,1,0:T(8,128)S(1)}, u32[]{:S(2)}, u32[]{:S(2)}) collective-permute-start(f32[2,64,256]{2,1,0:T(8,128)S(1)} %broadcast_select_fusion.5), channel_id=1, source_target_pairs={{0,1},{1,0},{2,3},{3,2},{4,5},{5,4},{6,7},{7,6},{8,9},{9,8},{10,11... | collective-permute-start | bytes 393224 | tf_op jit(solution)/shard_map/out6x/ppermute | solution.py:241
  64.1 0.0 collective-permute-done.19
  64.2 3.7 %collective-permute-start.20 = (f32[2,64,256]{2,1,0:T(8,128)S(1)}, f32[2,64,256]{2,1,0:T(8,128)S(1)}, u32[]{:S(2)}, u32[]{:S(2)}) collective-permute-start(f32[2,64,256]{2,1,0:T(8,128)S(1)} %add_select_fusion.4), channel_id=1, source_target_pairs={{0,1},{1,0},{2,3},{3,2},{4,5},{5,4},{6,7},{7,6},{8,9},{9,8},{10,11... | collective-permute-start | bytes 393224 | tf_op jit(solution)/shard_map/out8x/ppermute | solution.py:241
  67.9 1.4 %collective-permute-start.18 = (f32[2,64,256]{2,1,0:T(8,128)S(1)}, f32[2,64,256]{2,1,0:T(8,128)S(1)}, u32[]{:S(2)}, u32[]{:S(2)}) collective-permute-start(f32[2,64,256]{2,1,0:T(8,128)S(1)} %broadcast_select_fusion.4), channel_id=1, source_target_pairs={{0,1},{1,0},{2,3},{3,2},{4,5},{5,4},{6,7},{7,6},{8,9},{9,8},{10,11... | collective-permute-start | bytes 393224 | tf_op jit(solution)/shard_map/out7x/ppermute | solution.py:241
  69.2 0.0 collective-permute-done.16
  69.3 0.1 collective-permute-start.21
  69.4 3.5 %collective-permute-done.18 = f32[2,64,256]{2,1,0:T(8,128)S(1)} collective-permute-done((f32[2,64,256]{2,1,0:T(8,128)S(1)}, f32[2,64,256]{2,1,0:T(8,128)S(1)}, u32[]{:S(2)}, u32[]{:S(2)}) %collective-permute-start.18) | collective-permute-done | bytes 131104 | tf_op jit(solution)/shard_map/out7x/ppermute | solution.py:241
  72.9 0.1 collective-permute-start.23
  73.1 0.0 collective-permute-done.21
  73.1 3.5 %collective-permute-start.22 = (f32[2,64,256]{2,1,0:T(8,128)S(1)}, f32[2,64,256]{2,1,0:T(8,128)S(1)}, u32[]{:S(2)}, u32[]{:S(2)}) collective-permute-start(f32[2,64,256]{2,1,0:T(8,128)S(1)} %add_select_fusion.2), channel_id=1, source_target_pairs={{0,1},{1,0},{2,3},{3,2},{4,5},{5,4},{6,7},{7,6},{8,9},{9,8},{10,11... | collective-permute-start | bytes 393224 | tf_op jit(solution)/shard_map/out9x/ppermute | solution.py:241
  76.6 0.0 collective-permute-done.23
  76.6 3.0 %collective-permute-start.24 = (f32[2,64,256]{2,1,0:T(8,128)S(1)}, f32[2,64,256]{2,1,0:T(8,128)S(1)}, u32[]{:S(2)}, u32[]{:S(2)}) collective-permute-start(f32[2,64,256]{2,1,0:T(8,128)S(1)} %add_select_fusion), channel_id=1, source_target_pairs={{0,1},{1,0},{2,3},{3,2},{4,5},{5,4},{6,7},{7,6},{8,9},{9,8},{10,11... | collective-permute-start | bytes 393224 | tf_op jit(solution)/shard_map/out10x/ppermute | solution.py:241
  79.6 0.9 %collective-permute-done.22 = f32[2,64,256]{2,1,0:T(8,128)S(1)} collective-permute-done((f32[2,64,256]{2,1,0:T(8,128)S(1)}, f32[2,64,256]{2,1,0:T(8,128)S(1)}, u32[]{:S(2)}, u32[]{:S(2)}) %collective-permute-start.22) | collective-permute-done | bytes 131104 | tf_op jit(solution)/shard_map/out9x/ppermute | solution.py:241
  80.6 0.0 copy-start.2
  80.6 2.0 %collective-permute-done.24 = f32[2,64,256]{2,1,0:T(8,128)S(1)} collective-permute-done((f32[2,64,256]{2,1,0:T(8,128)S(1)}, f32[2,64,256]{2,1,0:T(8,128)S(1)}, u32[]{:S(2)}, u32[]{:S(2)}) %collective-permute-start.24) | collective-permute-done | bytes 131104 | tf_op jit(solution)/shard_map/out10x/ppermute | solution.py:241
  82.6 0.7 select_dynamic-update-slice_fusion
  (26 shorter events, 0.5 us)
Async XLA Ops:
  1.3 7.6 %collective-permute-start.1 = (f32[7,64,256]{2,1,0:T(8,128)S(1)}, f32[7,64,256]{2,1,0:T(8,128)S(1)}, u32[]{:S(2)}, u32[]{:S(2)}) collective-permute-start(f32[7,64,256]{2,1,0:T(8,128)S(1)} %get-tuple-element.43), channel_id=1, source_target_pairs={{0,4},{1,5},{2,6},{3,7},{4,0},{5,1},{6,2},{7,3},{8,12},{9,13},{10,... | collective-permute-start | bytes 1376264 | tf_op jit(solution)/shard_map/est_a/ppermute | solution.py:241
  1.8 9.1 %collective-permute-start = (f32[7,64,256]{2,1,0:T(8,128)S(1)}, f32[7,64,256]{2,1,0:T(8,128)S(1)}, u32[]{:S(2)}, u32[]{:S(2)}) collective-permute-start(f32[7,64,256]{2,1,0:T(8,128)S(1)} %get-tuple-element.44), channel_id=1, source_target_pairs={{0,1},{1,0},{2,3},{3,2},{4,8},{5,9},{6,10},{7,11},{8,4},{9,5},{10,... | collective-permute-start | bytes 1376264 | tf_op jit(solution)/shard_map/est_b/ppermute | solution.py:241
  4.5 1.2 %copy-start = (f32[16,64,256]{2,1,0:T(8,128)S(1)}, f32[16,64,256]{2,1,0:T(8,128)}, u32[]{:S(2)}) copy-start(f32[16,64,256]{2,1,0:T(8,128)} %est.3) | copy-start | bytes 3145732
  5.7 5.3 %copy-start.1 = (f32[2,16,64,256]{3,2,1,0:T(8,128)S(1)}, f32[2,16,64,256]{3,2,1,0:T(8,128)}, u32[]{:S(2)}) copy-start(f32[2,16,64,256]{3,2,1,0:T(8,128)} %measured.3) | copy-start | bytes 6291460
  16.8 9.2 %collective-permute-start.5 = (f32[7,64,256]{2,1,0:T(8,128)S(1)}, f32[7,64,256]{2,1,0:T(8,128)S(1)}, u32[]{:S(2)}, u32[]{:S(2)}) collective-permute-start(f32[7,64,256]{2,1,0:T(8,128)S(1)} %get-tuple-element.47), channel_id=1, source_target_pairs={{0,4},{1,5},{2,6},{3,7},{4,0},{5,1},{6,2},{7,3},{8,12},{9,13},{10,... | collective-permute-start | bytes 1376264 | tf_op jit(solution)/shard_map/ratio0_a/ppermute | solution.py:241
  16.9 9.1 %collective-permute-start.4 = (f32[7,64,256]{2,1,0:T(8,128)S(1)}, f32[7,64,256]{2,1,0:T(8,128)S(1)}, u32[]{:S(2)}, u32[]{:S(2)}) collective-permute-start(f32[7,64,256]{2,1,0:T(8,128)S(1)} %get-tuple-element.48), channel_id=1, source_target_pairs={{0,1},{1,0},{2,3},{3,2},{4,8},{5,9},{6,10},{7,11},{8,4},{9,5},{10,... | collective-permute-start | bytes 1376264 | tf_op jit(solution)/shard_map/ratio0_b/ppermute | solution.py:241
  24.9 6.0 %collective-permute-start.3 = (f32[7,64,256]{2,1,0:T(8,128)S(1)}, f32[7,64,256]{2,1,0:T(8,128)S(1)}, u32[]{:S(2)}, u32[]{:S(2)}) collective-permute-start(f32[7,64,256]{2,1,0:T(8,128)S(1)} %get-tuple-element.51), channel_id=1, source_target_pairs={{0,4},{1,5},{2,6},{3,7},{4,0},{5,1},{6,2},{7,3},{8,12},{9,13},{10,... | collective-permute-start | bytes 1376264 | tf_op jit(solution)/shard_map/ratio1_a/ppermute | solution.py:241
  24.9 8.5 %collective-permute-start.2 = (f32[7,64,256]{2,1,0:T(8,128)S(1)}, f32[7,64,256]{2,1,0:T(8,128)S(1)}, u32[]{:S(2)}, u32[]{:S(2)}) collective-permute-start(f32[7,64,256]{2,1,0:T(8,128)S(1)} %get-tuple-element.52), channel_id=1, source_target_pairs={{0,1},{1,0},{2,3},{3,2},{4,8},{5,9},{6,10},{7,11},{8,4},{9,5},{10,... | collective-permute-start | bytes 1376264 | tf_op jit(solution)/shard_map/ratio1_b/ppermute | solution.py:241
  34.9 11.3 %collective-permute-start.9 = (f32[2,64,256]{2,1,0:T(8,128)S(1)}, f32[2,64,256]{2,1,0:T(8,128)S(1)}, u32[]{:S(2)}, u32[]{:S(2)}) collective-permute-start(f32[2,64,256]{2,1,0:T(8,128)S(1)} %get-tuple-element.36.refs_9_), channel_id=1, source_target_pairs={{0,1},{1,0},{2,3},{3,2},{4,5},{5,4},{6,7},{7,6},{8,9},{9,8},{10,11... | collective-permute-start | bytes 393224 | tf_op jit(solution)/shard_map/out1x/ppermute | solution.py:241
  37.3 6.9 %collective-permute-start.6 = (f32[2,64,256]{2,1,0:T(8,128)S(1)}, f32[2,64,256]{2,1,0:T(8,128)S(1)}, u32[]{:S(2)}, u32[]{:S(2)}) collective-permute-start(f32[2,64,256]{2,1,0:T(8,128)S(1)} %get-tuple-element.35), channel_id=1, source_target_pairs={{0,1},{1,0},{2,3},{3,2},{4,5},{5,4},{6,7},{7,6},{8,9},{9,8},{10,11... | collective-permute-start | bytes 393224 | tf_op jit(solution)/shard_map/out0x/ppermute | solution.py:241
  38.4 7.7 %collective-permute-start.12 = (f32[2,64,256]{2,1,0:T(8,128)S(1)}, f32[2,64,256]{2,1,0:T(8,128)S(1)}, u32[]{:S(2)}, u32[]{:S(2)}) collective-permute-start(f32[2,64,256]{2,1,0:T(8,128)S(1)} %get-tuple-element.39), channel_id=1, source_target_pairs={{0,1},{1,0},{2,3},{3,2},{4,5},{5,4},{6,7},{7,6},{8,9},{9,8},{10,11... | collective-permute-start | bytes 393224 | tf_op jit(solution)/shard_map/out2x/ppermute | solution.py:241
  44.1 2.6 %collective-permute-start.7 = (f32[2,64,256]{2,1,0:T(8,128)S(1)}, f32[2,64,256]{2,1,0:T(8,128)S(1)}, u32[]{:S(2)}, u32[]{:S(2)}) collective-permute-start(f32[2,64,256]{2,1,0:T(8,128)S(1)} %add_select_fusion.15), channel_id=1, source_target_pairs={{0,4},{1,2},{2,1},{3,7},{4,0},{5,6},{6,5},{7,3},{8,12},{9,10},{10,... | collective-permute-start | bytes 393224 | tf_op jit(solution)/shard_map/mid0x/ppermute | solution.py:241
  46.1 5.2 %collective-permute-start.13 = (f32[2,64,256]{2,1,0:T(8,128)S(1)}, f32[2,64,256]{2,1,0:T(8,128)S(1)}, u32[]{:S(2)}, u32[]{:S(2)}) collective-permute-start(f32[2,64,256]{2,1,0:T(8,128)S(1)} %add_select_fusion.11), channel_id=1, source_target_pairs={{0,4},{1,2},{2,1},{3,7},{4,0},{5,6},{6,5},{7,3},{8,12},{9,10},{10,... | collective-permute-start | bytes 393224 | tf_op jit(solution)/shard_map/mid2x/ppermute | solution.py:241
  46.2 7.9 %collective-permute-start.10 = (f32[2,64,256]{2,1,0:T(8,128)S(1)}, f32[2,64,256]{2,1,0:T(8,128)S(1)}, u32[]{:S(2)}, u32[]{:S(2)}) collective-permute-start(f32[2,64,256]{2,1,0:T(8,128)S(1)} %add_select_fusion.13), channel_id=1, source_target_pairs={{0,4},{1,2},{2,1},{3,7},{4,0},{5,6},{6,5},{7,3},{8,12},{9,10},{10,... | collective-permute-start | bytes 393224 | tf_op jit(solution)/shard_map/mid1x/ppermute | solution.py:241
  46.8 9.2 %collective-permute-start.8 = (f32[2,64,256]{2,1,0:T(8,128)S(1)}, f32[2,64,256]{2,1,0:T(8,128)S(1)}, u32[]{:S(2)}, u32[]{:S(2)}) collective-permute-start(f32[2,64,256]{2,1,0:T(8,128)S(1)} %broadcast_select_fusion.8), channel_id=1, source_target_pairs={{0,1},{1,0},{2,3},{3,2},{4,5},{5,4},{6,7},{7,6},{8,9},{9,8},{10,11... | collective-permute-start | bytes 393224 | tf_op jit(solution)/shard_map/out3x/ppermute | solution.py:241
  51.3 8.6 %collective-permute-start.14 = (f32[2,64,256]{2,1,0:T(8,128)S(1)}, f32[2,64,256]{2,1,0:T(8,128)S(1)}, u32[]{:S(2)}, u32[]{:S(2)}) collective-permute-start(f32[2,64,256]{2,1,0:T(8,128)S(1)} %broadcast_select_fusion.6), channel_id=1, source_target_pairs={{0,1},{1,0},{2,3},{3,2},{4,5},{5,4},{6,7},{7,6},{8,9},{9,8},{10,11... | collective-permute-start | bytes 393224 | tf_op jit(solution)/shard_map/out5x/ppermute | solution.py:241
  54.1 5.7 %collective-permute-start.11 = (f32[2,64,256]{2,1,0:T(8,128)S(1)}, f32[2,64,256]{2,1,0:T(8,128)S(1)}, u32[]{:S(2)}, u32[]{:S(2)}) collective-permute-start(f32[2,64,256]{2,1,0:T(8,128)S(1)} %broadcast_select_fusion.7), channel_id=1, source_target_pairs={{0,1},{1,0},{2,3},{3,2},{4,5},{5,4},{6,7},{7,6},{8,9},{9,8},{10,11... | collective-permute-start | bytes 393224 | tf_op jit(solution)/shard_map/out4x/ppermute | solution.py:241
  56.1 4.5 %collective-permute-start.15 = (f32[2,64,256]{2,1,0:T(8,128)S(1)}, f32[2,64,256]{2,1,0:T(8,128)S(1)}, u32[]{:S(2)}, u32[]{:S(2)}) collective-permute-start(f32[2,64,256]{2,1,0:T(8,128)S(1)} %get-tuple-element.63), channel_id=1, source_target_pairs={{0,4},{1,2},{2,1},{3,7},{4,0},{5,6},{6,5},{7,3},{8,12},{9,10},{10,... | collective-permute-start | bytes 393224 | tf_op jit(solution)/shard_map/mid3x/ppermute | solution.py:241
  59.9 4.2 %collective-permute-start.19 = (f32[2,64,256]{2,1,0:T(8,128)S(1)}, f32[2,64,256]{2,1,0:T(8,128)S(1)}, u32[]{:S(2)}, u32[]{:S(2)}) collective-permute-start(f32[2,64,256]{2,1,0:T(8,128)S(1)} %get-tuple-element.59), channel_id=1, source_target_pairs={{0,4},{1,2},{2,1},{3,7},{4,0},{5,6},{6,5},{7,3},{8,12},{9,10},{10,... | collective-permute-start | bytes 393224 | tf_op jit(solution)/shard_map/mid5x/ppermute | solution.py:241
  60.0 7.8 %collective-permute-start.17 = (f32[2,64,256]{2,1,0:T(8,128)S(1)}, f32[2,64,256]{2,1,0:T(8,128)S(1)}, u32[]{:S(2)}, u32[]{:S(2)}) collective-permute-start(f32[2,64,256]{2,1,0:T(8,128)S(1)} %get-tuple-element.61), channel_id=1, source_target_pairs={{0,4},{1,2},{2,1},{3,7},{4,0},{5,6},{6,5},{7,3},{8,12},{9,10},{10,... | collective-permute-start | bytes 393224 | tf_op jit(solution)/shard_map/mid4x/ppermute | solution.py:241
  60.5 8.7 %collective-permute-start.16 = (f32[2,64,256]{2,1,0:T(8,128)S(1)}, f32[2,64,256]{2,1,0:T(8,128)S(1)}, u32[]{:S(2)}, u32[]{:S(2)}) collective-permute-start(f32[2,64,256]{2,1,0:T(8,128)S(1)} %broadcast_select_fusion.5), channel_id=1, source_target_pairs={{0,1},{1,0},{2,3},{3,2},{4,5},{5,4},{6,7},{7,6},{8,9},{9,8},{10,11... | collective-permute-start | bytes 393224 | tf_op jit(solution)/shard_map/out6x/ppermute | solution.py:241
  64.2 8.8 %collective-permute-start.20 = (f32[2,64,256]{2,1,0:T(8,128)S(1)}, f32[2,64,256]{2,1,0:T(8,128)S(1)}, u32[]{:S(2)}, u32[]{:S(2)}) collective-permute-start(f32[2,64,256]{2,1,0:T(8,128)S(1)} %add_select_fusion.4), channel_id=1, source_target_pairs={{0,1},{1,0},{2,3},{3,2},{4,5},{5,4},{6,7},{7,6},{8,9},{9,8},{10,11... | collective-permute-start | bytes 393224 | tf_op jit(solution)/shard_map/out8x/ppermute | solution.py:241
  67.9 5.0 %collective-permute-start.18 = (f32[2,64,256]{2,1,0:T(8,128)S(1)}, f32[2,64,256]{2,1,0:T(8,128)S(1)}, u32[]{:S(2)}, u32[]{:S(2)}) collective-permute-start(f32[2,64,256]{2,1,0:T(8,128)S(1)} %broadcast_select_fusion.4), channel_id=1, source_target_pairs={{0,1},{1,0},{2,3},{3,2},{4,5},{5,4},{6,7},{7,6},{8,9},{9,8},{10,11... | collective-permute-start | bytes 393224 | tf_op jit(solution)/shard_map/out7x/ppermute | solution.py:241
  69.3 3.8 %collective-permute-start.21 = (f32[2,64,256]{2,1,0:T(8,128)S(1)}, f32[2,64,256]{2,1,0:T(8,128)S(1)}, u32[]{:S(2)}, u32[]{:S(2)}) collective-permute-start(f32[2,64,256]{2,1,0:T(8,128)S(1)} %get-tuple-element.57), channel_id=1, source_target_pairs={{0,4},{1,2},{2,1},{3,7},{4,0},{5,6},{6,5},{7,3},{8,12},{9,10},{10,... | collective-permute-start | bytes 393224 | tf_op jit(solution)/shard_map/mid6x/ppermute | solution.py:241
  72.9 3.6 %collective-permute-start.23 = (f32[2,64,256]{2,1,0:T(8,128)S(1)}, f32[2,64,256]{2,1,0:T(8,128)S(1)}, u32[]{:S(2)}, u32[]{:S(2)}) collective-permute-start(f32[2,64,256]{2,1,0:T(8,128)S(1)} %get-tuple-element.55), channel_id=1, source_target_pairs={{0,4},{1,2},{2,1},{3,7},{4,0},{5,6},{6,5},{7,3},{8,12},{9,10},{10,... | collective-permute-start | bytes 393224 | tf_op jit(solution)/shard_map/mid7x/ppermute | solution.py:241
  73.1 7.5 %collective-permute-start.22 = (f32[2,64,256]{2,1,0:T(8,128)S(1)}, f32[2,64,256]{2,1,0:T(8,128)S(1)}, u32[]{:S(2)}, u32[]{:S(2)}) collective-permute-start(f32[2,64,256]{2,1,0:T(8,128)S(1)} %add_select_fusion.2), channel_id=1, source_target_pairs={{0,1},{1,0},{2,3},{3,2},{4,5},{5,4},{6,7},{7,6},{8,9},{9,8},{10,11... | collective-permute-start | bytes 393224 | tf_op jit(solution)/shard_map/out9x/ppermute | solution.py:241
  76.6 6.0 %collective-permute-start.24 = (f32[2,64,256]{2,1,0:T(8,128)S(1)}, f32[2,64,256]{2,1,0:T(8,128)S(1)}, u32[]{:S(2)}, u32[]{:S(2)}) collective-permute-start(f32[2,64,256]{2,1,0:T(8,128)S(1)} %add_select_fusion), channel_id=1, source_target_pairs={{0,1},{1,0},{2,3},{3,2},{4,5},{5,4},{6,7},{7,6},{8,9},{9,8},{10,11... | collective-permute-start | bytes 393224 | tf_op jit(solution)/shard_map/out10x/ppermute | solution.py:241
  80.6 2.0 %copy-start.2 = (f32[16,64,256]{2,1,0:T(8,128)}, f32[16,64,256]{2,1,0:T(8,128)S(1)}, u32[]{:S(2)}) copy-start(f32[16,64,256]{2,1,0:T(8,128)S(1)} %select_dynamic-update-slice_fusion.1) | copy-start | bytes 3145732
